TPU v7x, 32 devices: a whole 2x2x4 slice. The times are simulated.
32 devices in a mesh: grp: 2 (over x), seq: 8 (over z, y), mdl: 2 (over core).
Axes of the slice: x: 2, y: 2, z: 4, core: 2. Of those that a mesh axis runs over, the one named last changes fastest.
Arguments:
- signal: float32 [8, 128, 8192], P('grp', 'mdl', 'seq'), parts along dimension 0, may hold values from -6 to 6
- lengths: int32 [8], P('grp'), parts along dimension 0, may hold values from 1 to 64, 160 in all
- chan_weight: bfloat16 [128, 128, 16], P('mdl'), may hold values from -0.5 to 0.5
- up_weight: bfloat16 [4, 2048, 4096], P(None, 'seq', 'mdl'), may hold values from -0.125 to 0.125
- down_weight: bfloat16 [4, 2048, 4096], P(None, 'seq', 'mdl'), may hold values from -0.09375 to 0.09375
Outputs:
- features: bfloat16 [8, 64, 2048], P(('grp', 'mdl'), 'seq'), parts along dimension 0
There are 2 independent parts, one for each index of `grp`. A program takes and returns all parts, laid end to end along the dimension named above; an argument that names none is the same for every part. Nothing has to cross between parts.
Inputs may be any that keep to these rules, and one draw needn't show every extreme that they name: `lengths`: live windows of each recording; one recording is live for all 64, and all recordings together have (320) // 2.
All inputs are finite; a program needn't handle non-finite values.
Results may differ from a plain program's by a relative error of at most 0.014.
Values may be sent and summed in bfloat16 or wider, within the bound.
A program may use at most 128 MiB of HBM per device.

v0:
```python
import math

import jax
import jax.numpy as jnp
from jax import lax
from jax.sharding import PartitionSpec as P

HOP = 128


EPSILON = 1e-06


def shifted(x, axis, by):
    size = lax.axis_size(axis)
    pairs = [(i, i + by) for i in range(size) if 0 <= i + by < size]
    return lax.ppermute(x, axis, pairs)


def shifted_2(value, axis, steps):
    count = lax.axis_size(axis)
    pairs = [(source, (source + steps) % count) for source in range(count)]
    return lax.ppermute(value, axis, pairs)


def spectral_table(half_span):
    full_span = 2 * half_span
    row_index = jnp.arange(full_span, dtype=jnp.int32)
    col_index = jnp.arange(half_span, dtype=jnp.int32)
    phases = row_index[:, None] * col_index[None, :] % full_span
    angles = phases.astype(jnp.float32) * (2.0 * math.pi / full_span)
    window_taper = 0.5 - 0.5 * jnp.cos(row_index.astype(jnp.float32) * (2.0 * math.pi / full_span))
    weighting = window_taper * (1.0 / math.sqrt(full_span))
    joined = jnp.concatenate([jnp.cos(angles), -jnp.sin(angles)], axis=1) * weighting[:, None]
    return jnp.concatenate([joined[:half_span], joined[half_span:]], axis=1)


def log_power(spectrum):
    half_span = spectrum.shape[-1] // 2
    real_part = spectrum[..., :half_span]
    imag_part = spectrum[..., half_span:]
    return jnp.log1p(real_part * real_part + imag_part * imag_part).astype(jnp.bfloat16)


def normalize(state_rows):
    values = state_rows.astype(jnp.float32)
    scaled = values * lax.rsqrt(jnp.mean(values * values, axis=1, keepdims=True) + EPSILON)
    return (values, scaled.astype(jnp.bfloat16))


def project_down(hidden, own_down):
    return lax.dot_general(
        hidden, own_down, (((1,), (1,)), ((), ())), preferred_element_type=jnp.float32
    )


def apply_layer(state_rows, own_up, own_down):
    values, normed = normalize(state_rows)
    hidden = jax.nn.gelu(jnp.dot(normed, own_up, preferred_element_type=jnp.float32)).astype(
        jnp.bfloat16
    )
    summed = lax.psum(project_down(hidden, own_down), "mdl")
    return (values + summed).astype(jnp.bfloat16)


def body(signal, lengths, chan_weight, up_weight, down_weight):
    streams, channels, samples = signal.shape
    frames = samples // HOP
    dft_table = spectral_table(HOP)
    boundary = shifted(signal[:, :, :HOP], "seq", -1)
    local_part = jnp.dot(
        signal.reshape(streams, channels, frames, HOP), dft_table, precision=lax.Precision.HIGHEST
    )
    edge_part = jnp.dot(boundary, dft_table[:, 2 * HOP :], precision=lax.Precision.HIGHEST)
    following = jnp.concatenate([local_part[:, :, 1:, 2 * HOP :], edge_part[:, :, None, :]], axis=2)
    spectrum = local_part[..., : 2 * HOP] + following
    logpower = log_power(spectrum)
    embedded = jnp.einsum(
        "scfb,cbe->sfce", logpower, chan_weight, preferred_element_type=jnp.float32
    )
    embedded = embedded.reshape(streams, frames, channels * chan_weight.shape[2])
    frame_index = lax.axis_index("seq") * frames + jnp.arange(frames, dtype=jnp.int32)
    live_mask = frame_index[None, :] < lengths[:, None]
    tokens = jnp.where(live_mask[:, :, None], embedded, 0.0).astype(jnp.bfloat16)
    layer_count = up_weight.shape[0]
    group_size = lax.axis_size("seq") // layer_count
    own_up, own_down = (
        lax.all_to_all(
            jnp.repeat(up_weight, group_size, axis=0),
            "seq",
            split_axis=0,
            concat_axis=1,
            tiled=True,
        ),
        lax.all_to_all(
            jnp.repeat(down_weight, group_size, axis=0),
            "seq",
            split_axis=0,
            concat_axis=1,
            tiled=True,
        ),
    )
    own_up = own_up[0]
    own_down = own_down[0]
    layer_index = lax.axis_index("seq") // group_size
    state_rows = lax.all_gather(tokens, "mdl", axis=2, tiled=True)
    kept_shape = state_rows.shape
    state_rows = state_rows.reshape(kept_shape[0] * kept_shape[1], kept_shape[2])
    for turn_number in range(2 * layer_count):
        if turn_number < 2 * layer_count - 1:
            offset = turn_number - layer_index
            active = (offset >= 0) & (offset < layer_count)
            state_rows = jnp.where(active, apply_layer(state_rows, own_up, own_down), state_rows)
        state_rows = shifted_2(state_rows, "seq", group_size)
    full_rows = state_rows.reshape(kept_shape)
    half_streams = kept_shape[0] // lax.axis_size("mdl")
    return lax.dynamic_slice_in_dim(
        full_rows, lax.axis_index("mdl") * half_streams, half_streams, 0
    )


def solution(mesh):
    return jax.shard_map(
        body,
        mesh=mesh,
        in_specs=(
            P("grp", "mdl", "seq"),
            P("grp"),
            P("mdl", None, None),
            P(None, "seq", "mdl"),
            P(None, "seq", "mdl"),
        ),
        out_specs=P(("grp", "mdl"), "seq", None),
        check_vma=False,
    )
```

profile of v0, /device:TPU:0, one launch (start us, length us, event | category | flops | bytes accessed | tf_op | source)
XLA Modules:
  0.0 677.4 jit_solution(12882907544633261924)
XLA Ops:
  6.5 6.8 %broadcast_in_dim.22 = bf16[4,2,256,2048]{3,2,1,0:T(8,128)(2,1)} broadcast(bf16[4,256,2048]{2,1,0:T(8,128)(2,1)} %param.9), dimensions={0,2,3} | broadcast | bytes 12582912 | tf_op jit(solution)/shard_map/broadcast_in_dim | solution.py:96
  13.3 190.7 %all_to_all.8 = bf16[8,256,2048]{2,1,0:T(8,128)(2,1)} all-to-all(bf16[8,256,2048]{2,1,0:T(8,128)(2,1)} %bitcast.67), channel_id=1, replica_groups=mesh['grp'=2,'seq'=8,'mdl'=2] {'seq'}, dimensions={0} | all-to-all | bytes 16777216 | tf_op jit(solution)/shard_map/all_to_all | solution.py:95
  204.0 4.3 broadcast_in_dim.21
  208.3 5.2 all-to-all-start
  213.6 1.3 collective-permute-start
  214.9 0.5 sine_negate_fusion
  215.5 0.1 maximum_multiply_fusion
  215.6 3.5 convolution_bitcast_fusion
  219.2 2.0 copy-done.1
  221.1 0.2 slice.31
  221.4 42.6 %collective-permute-done = f32[4,64,128]{2,1,0:T(8,128)S(1)} collective-permute-done((f32[4,64,128]{2,1,0:T(8,128)S(1)}, f32[4,64,128]{2,1,0:T(8,128)S(1)}, u32[]{:S(2)}, u32[]{:S(2)}) %collective-permute-start) | collective-permute-done | bytes 131104 | tf_op jit(solution)/shard_map/ppermute | solution.py:17
  264.0 0.4 convolution_bitcast_fusion.2
  264.4 1.9 slice_add_fusion
  266.3 0.4 fusion.4
  266.8 0.4 convolution_bitcast_fusion.1
  267.2 0.2 copy.10
  267.4 0.8 reshape.133
  268.2 1.9 all_gather.3
  270.1 0.1 fusion.6
  270.3 126.8 %all-to-all-done = bf16[8,256,2048]{2,1,0:T(8,128)(2,1)} async-done(((bf16[8,256,2048]{2,1,0:T(8,128)(2,1)}), bf16[8,256,2048]{2,1,0:T(8,128)(2,1)}, u32[]{:S(2)}, u32[]{:S(2)}) %all-to-all-start) | async-done | bytes 8388640 | tf_op jit(solution)/shard_map/all_to_all | solution.py:88
  397.1 10.6 %fusion.143 = f32[32,2048]{1,0:T(8,128)} fusion(bf16[2048,2048]{1,0:T(8,128)(2,1)} %bitcast.59, bf16[2048,2048]{1,0:T(8,128)(2,1)} %bitcast.12, bf16[4,8,2048]{2,1,0:T(8,128)(2,1)S(1)} %all_gather.3, f32[4,8]{1,0:T(4,128)S(1)} %add_rsqrt_fusion), kind=kOutput, calls=%fused_computation.146 | convolution fusion | flops 537657344 | bytes 17170560 | tf_op jit(solution)/shard_map/dot_general | solution.py:52
  407.7 0.2 all-reduce.10.cloned.1.call-start
  407.9 23.9 %all-reduce.8.cloned.1.call-done = f32[32,2048]{1,0:T(8,128)} async-done(((f32[32,2048]{1,0:T(8,128)}), f32[32,2048]{1,0:T(8,128)}) %all-reduce.8.cloned.1.call-update) | async-done | bytes 262160 | tf_op jit(solution)/shard_map/psum | solution.py:62
  431.8 1.0 fusion.85
  432.8 1.8 collective-permute-start.1
  434.6 5.8 collective-permute-done.1
  440.4 0.1 fusion.16
  440.6 10.6 %fusion.135 = f32[32,2048]{1,0:T(8,128)} fusion(bf16[2048,2048]{1,0:T(8,128)(2,1)} %bitcast.60, bf16[2048,2048]{1,0:T(8,128)(2,1)} %bitcast.12, bf16[32,2048]{1,0:T(8,128)(2,1)S(1)} %collective-permute-done.1, f32[32]{0:T(128)S(1)} %add_rsqrt_fusion.6), kind=kOutput, calls=%fused_computation.144 | convolution fusion | flops 537657344 | bytes 17170560 | tf_op jit(solution)/shard_map/dot_general | solution.py:52
  451.2 17.7 %all-reduce.10.cloned.1.call-done = f32[32,2048]{1,0:T(8,128)} async-done(((f32[32,2048]{1,0:T(8,128)}), f32[32,2048]{1,0:T(8,128)}) %all-reduce.10.cloned.1.call-update) | async-done | bytes 262160 | tf_op jit(solution)/shard_map/psum | solution.py:62
  468.9 1.0 fusion.91
  469.9 1.8 collective-permute-start.2
  471.7 5.8 collective-permute-done.2
  477.5 0.1 fusion.27
  477.7 10.6 %fusion.127 = f32[32,2048]{1,0:T(8,128)} fusion(bf16[2048,2048]{1,0:T(8,128)(2,1)} %bitcast.61, bf16[2048,2048]{1,0:T(8,128)(2,1)} %bitcast.12, bf16[32,2048]{1,0:T(8,128)(2,1)S(1)} %collective-permute-done.2, f32[32]{0:T(128)S(1)} %add_rsqrt_fusion.5), kind=kOutput, calls=%fused_computation.142 | convolution fusion | flops 537657344 | bytes 17170560 | tf_op jit(solution)/shard_map/dot_general | solution.py:52
  488.3 17.7 %all-reduce.12.cloned.1.call-done = f32[32,2048]{1,0:T(8,128)} async-done(((f32[32,2048]{1,0:T(8,128)}), f32[32,2048]{1,0:T(8,128)}) %all-reduce.12.cloned.1.call-update) | async-done | bytes 262160 | tf_op jit(solution)/shard_map/psum | solution.py:62
  506.0 1.0 fusion.90
  507.0 1.8 collective-permute-start.3
  508.8 5.8 collective-permute-done.3
  514.6 0.1 fusion.38
  514.7 10.6 %fusion.119 = f32[32,2048]{1,0:T(8,128)} fusion(bf16[2048,2048]{1,0:T(8,128)(2,1)} %bitcast.62, bf16[2048,2048]{1,0:T(8,128)(2,1)} %bitcast.12, bf16[32,2048]{1,0:T(8,128)(2,1)S(1)} %collective-permute-done.3, f32[32]{0:T(128)S(1)} %add_rsqrt_fusion.4), kind=kOutput, calls=%fused_computation.140 | convolution fusion | flops 537657344 | bytes 17170560 | tf_op jit(solution)/shard_map/dot_general | solution.py:52
  525.4 17.7 %all-reduce.14.cloned.1.call-done = f32[32,2048]{1,0:T(8,128)} async-done(((f32[32,2048]{1,0:T(8,128)}), f32[32,2048]{1,0:T(8,128)}) %all-reduce.14.cloned.1.call-update) | async-done | bytes 262160 | tf_op jit(solution)/shard_map/psum | solution.py:62
  543.1 1.0 fusion.89
  544.1 2.0 collective-permute-start.4
  546.1 5.8 collective-permute-done.4
  551.9 0.1 fusion.49
  552.0 10.6 %fusion.111 = f32[32,2048]{1,0:T(8,128)} fusion(bf16[2048,2048]{1,0:T(8,128)(2,1)} %bitcast.63, bf16[2048,2048]{1,0:T(8,128)(2,1)} %bitcast.12, bf16[32,2048]{1,0:T(8,128)(2,1)S(1)} %collective-permute-done.4, f32[32]{0:T(128)S(1)} %add_rsqrt_fusion.3), kind=kOutput, calls=%fused_computation.138 | convolution fusion | flops 537657344 | bytes 17170560 | tf_op jit(solution)/shard_map/dot_general | solution.py:52
  562.7 17.7 %all-reduce.16.cloned.1.call-done = f32[32,2048]{1,0:T(8,128)} async-done(((f32[32,2048]{1,0:T(8,128)}), f32[32,2048]{1,0:T(8,128)}) %all-reduce.16.cloned.1.call-update) | async-done | bytes 262160 | tf_op jit(solution)/shard_map/psum | solution.py:62
  580.4 1.0 fusion.88
  581.4 1.8 collective-permute-start.5
  583.2 5.8 collective-permute-done.5
  589.0 0.1 fusion.60
  589.1 10.6 %fusion.103 = f32[32,2048]{1,0:T(8,128)} fusion(bf16[2048,2048]{1,0:T(8,128)(2,1)} %bitcast.64, bf16[2048,2048]{1,0:T(8,128)(2,1)} %bitcast.12, bf16[32,2048]{1,0:T(8,128)(2,1)S(1)} %collective-permute-done.5, f32[32]{0:T(128)S(1)} %add_rsqrt_fusion.2), kind=kOutput, calls=%fused_computation.136 | convolution fusion | flops 537657344 | bytes 17170560 | tf_op jit(solution)/shard_map/dot_general | solution.py:52
  599.8 17.7 %all-reduce.18.cloned.1.call-done = f32[32,2048]{1,0:T(8,128)} async-done(((f32[32,2048]{1,0:T(8,128)}), f32[32,2048]{1,0:T(8,128)}) %all-reduce.18.cloned.1.call-update) | async-done | bytes 262160 | tf_op jit(solution)/shard_map/psum | solution.py:62
  617.5 1.0 fusion.87
  618.5 1.8 collective-permute-start.6
  620.3 5.8 collective-permute-done.6
  626.1 0.1 fusion.71
  626.2 10.6 %fusion.95 = f32[32,2048]{1,0:T(8,128)} fusion(bf16[2048,2048]{1,0:T(8,128)(2,1)} %bitcast.65, bf16[2048,2048]{1,0:T(8,128)(2,1)} %bitcast.12, bf16[32,2048]{1,0:T(8,128)(2,1)S(1)} %collective-permute-done.6, f32[32]{0:T(128)S(1)} %add_rsqrt_fusion.1), kind=kOutput, calls=%fused_computation.134 | convolution fusion | flops 537657344 | bytes 17170560 | tf_op jit(solution)/shard_map/dot_general | solution.py:52
  636.8 17.7 %all-reduce.20.cloned.1.call-done = f32[32,2048]{1,0:T(8,128)} async-done(((f32[32,2048]{1,0:T(8,128)}), f32[32,2048]{1,0:T(8,128)}) %all-reduce.20.cloned.1.call-update) | async-done | bytes 262160 | tf_op jit(solution)/shard_map/psum | solution.py:62
  654.6 1.0 fusion.86
  655.5 1.8 collective-permute-start.7
  657.3 5.8 collective-permute-done.7
  663.1 6.8 collective-permute-done.8
  669.9 0.6 constant_dynamic-slice_fusion
  (36 shorter events, 0.7 us)
Async XLA Ops:
  6.5 260.2 %copy-start = (bf16[64,128,16]{1,2,0:T(8,128)(2,1)S(1)}, bf16[64,128,16]{1,2,0:T(8,128)(2,1)}, u32[]{:S(2)}) copy-start(bf16[64,128,16]{1,2,0:T(8,128)(2,1)} %param.7) | copy-start | bytes 786436
  13.3 190.7 %copy-start.2 = (bf16[4,256,2048]{2,1,0:T(8,128)(2,1)S(1)}, bf16[4,256,2048]{2,1,0:T(8,128)(2,1)}, u32[]{:S(2)}) copy-start(bf16[4,256,2048]{2,1,0:T(8,128)(2,1)} %param.8) | copy-start | bytes 12582916
  208.3 5.2 copy-start.3
  208.3 188.8 %all-to-all-start = ((bf16[8,256,2048]{2,1,0:T(8,128)(2,1)}), bf16[8,256,2048]{2,1,0:T(8,128)(2,1)}, u32[]{:S(2)}, u32[]{:S(2)}) async-start(bf16[8,256,2048]{2,1,0:T(8,128)(2,1)} %bitcast.66), calls=%async_computation | async-start | bytes 16777216 | tf_op jit(solution)/shard_map/all_to_all | solution.py:88
  213.5 7.9 %copy-start.4 = (s32[4]{0:T(128)S(1)}, s32[4]{0:T(128)}, u32[]{:S(2)}) copy-start(s32[4]{0:T(128)} %param.6) | copy-start | bytes 52
  213.5 218.4 %all-reduce.8.cloned.1.call-start = ((), (), s32[]{:S(2)}) async-start(), calls=%async_computation.2 | async-start | bytes 524288 | tf_op jit(solution)/shard_map/psum | solution.py:62
  213.6 50.4 %collective-permute-start = (f32[4,64,128]{2,1,0:T(8,128)S(1)}, f32[4,64,128]{2,1,0:T(8,128)S(1)}, u32[]{:S(2)}, u32[]{:S(2)}) collective-permute-start(f32[4,64,128]{2,1,0:T(8,128)S(1)} %slice.25), channel_id=1, source_target_pairs={{2,0},{4,2},{6,4},{8,6},{10,8},{12,10},{14,12},{3,1},{5,3},{7,5},{... | collective-permute-start | bytes 393224 | tf_op jit(solution)/shard_map/ppermute | solution.py:17
  219.2 2.0 copy-start.1
  407.7 61.3 %all-reduce.10.cloned.1.call-start = ((), (), s32[]{:S(2)}) async-start(), calls=%async_computation.3 | async-start | bytes 524288 | tf_op jit(solution)/shard_map/psum | solution.py:62
  432.8 7.6 %collective-permute-start.1 = (bf16[32,2048]{1,0:T(8,128)(2,1)S(1)}, bf16[32,2048]{1,0:T(8,128)(2,1)S(1)}, u32[]{:S(2)}, u32[]{:S(2)}) collective-permute-start(bf16[32,2048]{1,0:T(8,128)(2,1)S(1)} %fusion.85), channel_id=1, source_target_pairs={{0,4},{2,6},{4,8},{6,10},{8,12},{10,14},{12,0},{14,2},{1,5},{3,7},... | collective-permute-start | bytes 393224 | tf_op jit(solution)/shard_map/ppermute | solution.py:23
  451.2 54.8 %all-reduce.12.cloned.1.call-start = ((), (), s32[]{:S(2)}) async-start(), calls=%async_computation.4 | async-start | bytes 524288 | tf_op jit(solution)/shard_map/psum | solution.py:62
  469.9 7.6 %collective-permute-start.2 = (bf16[32,2048]{1,0:T(8,128)(2,1)S(1)}, bf16[32,2048]{1,0:T(8,128)(2,1)S(1)}, u32[]{:S(2)}, u32[]{:S(2)}) collective-permute-start(bf16[32,2048]{1,0:T(8,128)(2,1)S(1)} %fusion.91), channel_id=1, source_target_pairs={{0,4},{2,6},{4,8},{6,10},{8,12},{10,14},{12,0},{14,2},{1,5},{3,7},... | collective-permute-start | bytes 393224 | tf_op jit(solution)/shard_map/ppermute | solution.py:23
  488.3 54.8 %all-reduce.14.cloned.1.call-start = ((), (), s32[]{:S(2)}) async-start(), calls=%async_computation.5 | async-start | bytes 524288 | tf_op jit(solution)/shard_map/psum | solution.py:62
  507.0 7.6 %collective-permute-start.3 = (bf16[32,2048]{1,0:T(8,128)(2,1)S(1)}, bf16[32,2048]{1,0:T(8,128)(2,1)S(1)}, u32[]{:S(2)}, u32[]{:S(2)}) collective-permute-start(bf16[32,2048]{1,0:T(8,128)(2,1)S(1)} %fusion.90), channel_id=1, source_target_pairs={{0,4},{2,6},{4,8},{6,10},{8,12},{10,14},{12,0},{14,2},{1,5},{3,7},... | collective-permute-start | bytes 393224 | tf_op jit(solution)/shard_map/ppermute | solution.py:23
  525.4 55.0 %all-reduce.16.cloned.1.call-start = ((), (), s32[]{:S(2)}) async-start(), calls=%async_computation.6 | async-start | bytes 524288 | tf_op jit(solution)/shard_map/psum | solution.py:62
  544.1 7.8 %collective-permute-start.4 = (bf16[32,2048]{1,0:T(8,128)(2,1)S(1)}, bf16[32,2048]{1,0:T(8,128)(2,1)S(1)}, u32[]{:S(2)}, u32[]{:S(2)}) collective-permute-start(bf16[32,2048]{1,0:T(8,128)(2,1)S(1)} %fusion.89), channel_id=1, source_target_pairs={{0,4},{2,6},{4,8},{6,10},{8,12},{10,14},{12,0},{14,2},{1,5},{3,7},... | collective-permute-start | bytes 393224 | tf_op jit(solution)/shard_map/ppermute | solution.py:23
  562.7 54.8 %all-reduce.18.cloned.1.call-start = ((), (), s32[]{:S(2)}) async-start(), calls=%async_computation.7 | async-start | bytes 524288 | tf_op jit(solution)/shard_map/psum | solution.py:62
  581.4 7.6 %collective-permute-start.5 = (bf16[32,2048]{1,0:T(8,128)(2,1)S(1)}, bf16[32,2048]{1,0:T(8,128)(2,1)S(1)}, u32[]{:S(2)}, u32[]{:S(2)}) collective-permute-start(bf16[32,2048]{1,0:T(8,128)(2,1)S(1)} %fusion.88), channel_id=1, source_target_pairs={{0,4},{2,6},{4,8},{6,10},{8,12},{10,14},{12,0},{14,2},{1,5},{3,7},... | collective-permute-start | bytes 393224 | tf_op jit(solution)/shard_map/ppermute | solution.py:23
  599.7 54.8 %all-reduce.20.cloned.1.call-start = ((), (), s32[]{:S(2)}) async-start(), calls=%async_computation.8 | async-start | bytes 524288 | tf_op jit(solution)/shard_map/psum | solution.py:62
  618.5 7.6 %collective-permute-start.6 = (bf16[32,2048]{1,0:T(8,128)(2,1)S(1)}, bf16[32,2048]{1,0:T(8,128)(2,1)S(1)}, u32[]{:S(2)}, u32[]{:S(2)}) collective-permute-start(bf16[32,2048]{1,0:T(8,128)(2,1)S(1)} %fusion.87), channel_id=1, source_target_pairs={{0,4},{2,6},{4,8},{6,10},{8,12},{10,14},{12,0},{14,2},{1,5},{3,7},... | collective-permute-start | bytes 393224 | tf_op jit(solution)/shard_map/ppermute | solution.py:23
  655.5 7.6 %collective-permute-start.7 = (bf16[32,2048]{1,0:T(8,128)(2,1)S(1)}, bf16[32,2048]{1,0:T(8,128)(2,1)S(1)}, u32[]{:S(2)}, u32[]{:S(2)}) collective-permute-start(bf16[32,2048]{1,0:T(8,128)(2,1)S(1)} %fusion.86), channel_id=1, source_target_pairs={{0,4},{2,6},{4,8},{6,10},{8,12},{10,14},{12,0},{14,2},{1,5},{3,7},... | collective-permute-start | bytes 393224 | tf_op jit(solution)/shard_map/ppermute | solution.py:23
  663.1 6.8 collective-permute-start.8
Sparse Core Ops, SparseCore 0:
  407.8 24.0 all-reduce.7
  451.3 17.5 all-reduce.9
  488.4 17.5 all-reduce.11
  525.5 17.5 all-reduce.13
  562.8 17.5 all-reduce.15
  599.9 17.5 all-reduce.17
  636.9 17.5 all-reduce.19
where the time goes:
time: 678 us; the launch traced here: 677 us
  waiting for transfers between devices  347 us (51%)
  blocking collectives  193 us (28%)
  matrix products  78.4 us (12%)
  starting transfers between devices  19.7 us (3%)
  local copies, waits for them, and re-layouts  14.9 us (2%)
  between operations  13.8 us (2%)
  other arithmetic  11.1 us (2%)
    all_to_all x1, blocking collectives, body(): lax.all_to_all(jnp.repeat(down_weight, group_size, axis=0), 'seq', split_...  191 us
    psum x7, waiting for transfers between devices, apply_layer(): summed = lax.psum(project_down(hidden, own_down), 'mdl')  130 us
    all_to_all x1, waiting for transfers between devices, body(): lax.all_to_all(jnp.repeat(up_weight, group_size, axis=0), 'seq', split_ax...  127 us
    dot_general x7, matrix products, project_down(): lax.dot_general(hidden, own_down, (((1,), (1,)), ((), ())), preferred_ele...  74.1 us
    ppermute x8, waiting for transfers between devices, shifted_2(): return lax.ppermute(value, axis, pairs)  47.4 us
    ppermute x1, waiting for transfers between devices, shifted(): return lax.ppermute(x, axis, pairs)  42.6 us
  transfers between devices with their start and end apart: 17, of which 17 were waited for; matrix products, arithmetic and copies ran while one was open for 1% of the time, Pallas kernels for 0%

commit v1 on v0

v1 whole, which is shorter than its diff:
```python
import math

import jax
import jax.numpy as jnp
from jax import lax
from jax.sharding import PartitionSpec as P

HOP = 128


EPSILON = 1e-06


def shifted(x, axis, by):
    size = lax.axis_size(axis)
    pairs = [(i, i + by) for i in range(size) if 0 <= i + by < size]
    return lax.ppermute(x, axis, pairs)


def spectral_table(half_span):
    full_span = 2 * half_span
    row_index = jnp.arange(full_span, dtype=jnp.int32)
    col_index = jnp.arange(half_span, dtype=jnp.int32)
    phases = row_index[:, None] * col_index[None, :] % full_span
    angles = phases.astype(jnp.float32) * (2.0 * math.pi / full_span)
    window_taper = 0.5 - 0.5 * jnp.cos(row_index.astype(jnp.float32) * (2.0 * math.pi / full_span))
    weighting = window_taper * (1.0 / math.sqrt(full_span))
    joined = jnp.concatenate([jnp.cos(angles), -jnp.sin(angles)], axis=1) * weighting[:, None]
    return jnp.concatenate([joined[:half_span], joined[half_span:]], axis=1)


def log_power(spectrum):
    half_span = spectrum.shape[-1] // 2
    real_part = spectrum[..., :half_span]
    imag_part = spectrum[..., half_span:]
    return jnp.log1p(real_part * real_part + imag_part * imag_part).astype(jnp.bfloat16)


def project_down(hidden, own_down):
    return lax.dot_general(
        hidden, own_down, (((1,), (1,)), ((), ())), preferred_element_type=jnp.float32
    )


def apply_layer(state, up_rows, down_rows, width):
    values = state.astype(jnp.float32)
    squares = lax.psum(jnp.sum(values * values, axis=1, keepdims=True), "seq")
    partial = jnp.dot(state, up_rows, preferred_element_type=jnp.float32).astype(jnp.bfloat16)
    summed = lax.psum_scatter(partial, "seq", scatter_dimension=1, tiled=True)
    scale = lax.rsqrt(squares * (1.0 / width) + EPSILON)
    hidden = jax.nn.gelu(summed.astype(jnp.float32) * scale).astype(jnp.bfloat16)
    hidden = lax.all_gather(hidden, "seq", axis=1, tiled=True)
    added = lax.psum(project_down(hidden, down_rows), "mdl")
    return (values + added).astype(jnp.bfloat16)


def body(signal, lengths, chan_weight, up_weight, down_weight):
    streams, channels, samples = signal.shape
    frames = samples // HOP
    dft_table = spectral_table(HOP)
    boundary = shifted(signal[:, :, :HOP], "seq", -1)
    local_part = jnp.dot(
        signal.reshape(streams, channels, frames, HOP), dft_table, precision=lax.Precision.HIGHEST
    )
    edge_part = jnp.dot(boundary, dft_table[:, 2 * HOP :], precision=lax.Precision.HIGHEST)
    following = jnp.concatenate([local_part[:, :, 1:, 2 * HOP :], edge_part[:, :, None, :]], axis=2)
    spectrum = local_part[..., : 2 * HOP] + following
    logpower = log_power(spectrum)
    embedded = jnp.einsum(
        "scfb,cbe->sfce", logpower, chan_weight, preferred_element_type=jnp.float32
    )
    embedded = embedded.reshape(streams, frames, channels * chan_weight.shape[2])
    frame_index = lax.axis_index("seq") * frames + jnp.arange(frames, dtype=jnp.int32)
    live_mask = frame_index[None, :] < lengths[:, None]
    tokens = jnp.where(live_mask[:, :, None], embedded, 0.0).astype(jnp.bfloat16)
    rows = lax.all_gather(tokens.reshape(streams * frames, -1), "mdl", axis=1, tiled=True)
    state = lax.all_to_all(rows, "seq", split_axis=1, concat_axis=0, tiled=True)
    width = rows.shape[1]
    for layer in range(up_weight.shape[0]):
        state = apply_layer(state, up_weight[layer], down_weight[layer], width)
    rows = lax.all_to_all(state, "seq", split_axis=0, concat_axis=1, tiled=True)
    full_rows = rows.reshape(streams, frames, width)
    half_streams = streams // lax.axis_size("mdl")
    return lax.dynamic_slice_in_dim(
        full_rows, lax.axis_index("mdl") * half_streams, half_streams, 0
    )


def solution(mesh):
    return jax.shard_map(
        body,
        mesh=mesh,
        in_specs=(
            P("grp", "mdl", "seq"),
            P("grp"),
            P("mdl", None, None),
            P(None, "seq", "mdl"),
            P(None, "seq", "mdl"),
        ),
        out_specs=P(("grp", "mdl"), "seq", None),
        check_vma=False,
    )
```

time: 678 us -> 577 us (0.85)
  blocking collectives: 193 us -> 101 us
  waiting for transfers between devices: 347 us -> 407 us
  matrix products: 78.4 us -> 27.1 us
  starting transfers between devices: 19.7 us -> 7.53 us
  local copies, waits for them, and re-layouts: 14.9 us -> 5.18 us
    all_to_all x1, blocking collectives: 191 us -> 15.4 us  [body(): state = lax.all_to_all(rows, 'seq', split_axis=1, concat_axis=0, tiled=True)]
    reduce_scatter x0 -> x4, waiting for transfers between devices: none -> 174 us  [apply_layer(): summed = lax.psum_scatter(partial, 'seq', scatter_dimension=1, tiled=True)]
    all_gather x0 -> x4, waiting for transfers between devices: none -> 156 us  [apply_layer(): hidden = lax.all_gather(hidden, 'seq', axis=1, tiled=True)]
    all_to_all x1, waiting for transfers between devices: 127 us -> 7.45 us  [body(): rows = lax.all_to_all(state, 'seq', split_axis=0, concat_axis=1, tiled=True)]
    psum x0 -> x4, blocking collectives: none -> 83.7 us  [apply_layer(): squares = lax.psum(jnp.sum(values * values, axis=1, keepdims=True), 'seq')]
    dot_general x7 -> x4, matrix products: 74.1 us -> 10.9 us  [project_down(): lax.dot_general(hidden, own_down, (((1,), (1,)), ((), ())), preferred_ele...]
    psum x7 -> x4, waiting for transfers between devices: 130 us -> 69.1 us  [apply_layer(): added = lax.psum(project_down(hidden, down_rows), 'mdl')]
    ppermute x8 -> x0, waiting for transfers between devices: 47.4 us -> none  [shifted_2(): return lax.ppermute(value, axis, pairs)]
  transfers between devices with their start and end apart: 17 -> 14, of which waited for: 17 -> 13; matrix products, arithmetic and copies ran while one was open for 1% -> 1% of each run, Pallas kernels for 0% -> 0%
where the time goes in v1:
time: 577 us; the launch traced here: 576 us
  waiting for transfers between devices  407 us (71%)
  blocking collectives  101 us (18%)
  matrix products  27.1 us (5%)
  other arithmetic  15 us (3%)
  between operations  13.7 us (2%)
  starting transfers between devices  7.53 us (1%)
    reduce_scatter x4, waiting for transfers between devices, apply_layer(): summed = lax.psum_scatter(partial, 'seq', scatter_dimension=1, tiled=True)  174 us
    all_gather x4, waiting for transfers between devices, apply_layer(): hidden = lax.all_gather(hidden, 'seq', axis=1, tiled=True)  156 us
    psum x4, blocking collectives, apply_layer(): squares = lax.psum(jnp.sum(values * values, axis=1, keepdims=True), 'seq')  83.7 us
    psum x4, waiting for transfers between devices, apply_layer(): added = lax.psum(project_down(hidden, down_rows), 'mdl')  69.1 us
    all_to_all x1, blocking collectives, body(): state = lax.all_to_all(rows, 'seq', split_axis=1, concat_axis=0, tiled=True)  15.4 us
  transfers between devices with their start and end apart: 14, of which 13 were waited for; matrix products, arithmetic and copies ran while one was open for 1% of the time, Pallas kernels for 0%

profile of v1, /device:TPU:0, one launch (start us, length us, event | category | flops | bytes accessed | tf_op | source)
XLA Modules:
  0.0 576.4 jit_solution(18243975974515709880)
XLA Ops:
  6.5 1.0 slice.49
  7.5 1.3 collective-permute-start
  8.8 0.5 sine_negate_fusion
  9.4 0.1 maximum_multiply_fusion
  9.5 4.7 convolution_bitcast_fusion
  14.3 1.9 copy-done.1
  16.2 0.2 slice.63
  16.4 0.1 lt.33
  16.5 0.1 lt.34
  16.6 0.1 lt.35
  16.7 0.4 convolution_bitcast_fusion.2
  17.1 1.9 slice_add_fusion
  19.0 0.4 fusion.4
  19.4 0.4 convolution_bitcast_fusion.1
  19.9 0.2 copy.22
  20.1 0.8 reshape.60
  20.8 0.1 select_convert_fusion
  20.9 2.0 all_gather.15
  22.9 15.4 %all_to_all.35 = bf16[32,8,256]{2,0,1:T(8,128)(2,1)S(1)} all-to-all(bf16[32,8,256]{2,0,1:T(8,128)(2,1)S(1)} %bitcast.87), channel_id=1, replica_groups=mesh['grp'=2,'seq'=8,'mdl'=2] {'seq'}, dimensions={1} | all-to-all | bytes 262144 | tf_op jit(solution)/shard_map/all_to_all | solution.py:77
  38.4 2.7 convolution_convert_fusion.3
  41.0 0.0 all-gather.5.cloned.1.call-start
  41.1 0.1 multiply_reduce_fusion
  41.2 0.1 broadcast_in_dim.36
  41.3 18.6 %psum.56 = f32[256,1]{0,1:T(1,128)S(1)} all-reduce(f32[256,1]{0,1:T(1,128)S(1)} %broadcast_in_dim.36), channel_id=1, replica_groups=mesh['grp'=2,'seq'=8,'mdl'=2] {'seq'}, use_global_device_ids=true, to_apply=%region_2.3 | all-reduce | flops 256 | bytes 2048 | tf_op jit(solution)/shard_map/psum | solution.py:47
  59.9 43.4 %reduce-scatter.5.cloned.1.call-done = bf16[256,256]{1,0:T(8,128)(2,1)} async-done(((bf16[256,2048]{1,0:T(8,128)(2,1)}), bf16[256,256]{1,0:T(8,128)(2,1)}) %reduce-scatter.5.cloned.1.call-update) | async-done | bytes 131088 | tf_op jit(solution)/shard_map/reduce_scatter | solution.py:49
  103.2 1.7 fusion.39
  105.0 0.0 all-reduce.5.cloned.1.call-start
  105.0 39.1 %all-gather.5.cloned.1.call-done = bf16[256,2048]{1,0:T(8,128)(2,1)} async-done(((bf16[256,256]{1,0:T(8,128)(2,1)}), bf16[256,2048]{1,0:T(8,128)(2,1)}) %all-gather.5.cloned.1.call-update) | async-done | bytes 1048592 | tf_op jit(solution)/shard_map/all_gather | solution.py:52
  144.1 2.7 fusion.14
  146.9 17.3 %all-reduce.5.cloned.1.call-done = f32[256,256]{1,0:T(8,128)} async-done(((f32[256,256]{1,0:T(8,128)}), f32[256,256]{1,0:T(8,128)}) %all-reduce.5.cloned.1.call-update) | async-done | bytes 262160 | tf_op jit(solution)/shard_map/psum | solution.py:53
  164.2 1.1 fusion.26
  165.2 2.7 convolution_convert_fusion.2
  167.9 0.0 all-gather.7.cloned.1.call-start
  168.0 21.7 %psum.58 = f32[256,1]{0,1:T(1,128)S(1)} all-reduce(f32[256,1]{0,1:T(1,128)S(1)} %bitcast.88), channel_id=1, replica_groups=mesh['grp'=2,'seq'=8,'mdl'=2] {'seq'}, use_global_device_ids=true, to_apply=%region_6.7 | all-reduce | flops 256 | bytes 2048 | tf_op jit(solution)/shard_map/psum | solution.py:47
  189.7 43.6 %reduce-scatter.7.cloned.1.call-done = bf16[256,256]{1,0:T(8,128)(2,1)} async-done(((bf16[256,2048]{1,0:T(8,128)(2,1)}), bf16[256,256]{1,0:T(8,128)(2,1)}) %reduce-scatter.7.cloned.1.call-update) | async-done | bytes 131088 | tf_op jit(solution)/shard_map/reduce_scatter | solution.py:49
  233.3 1.7 fusion.47
  235.0 0.0 all-reduce.7.cloned.1.call-start
  235.1 38.8 %all-gather.7.cloned.1.call-done = bf16[256,2048]{1,0:T(8,128)(2,1)} async-done(((bf16[256,256]{1,0:T(8,128)(2,1)}), bf16[256,2048]{1,0:T(8,128)(2,1)}) %all-gather.7.cloned.1.call-update) | async-done | bytes 1048592 | tf_op jit(solution)/shard_map/all_gather | solution.py:52
  273.9 2.7 fusion.11
  276.7 17.3 %all-reduce.7.cloned.1.call-done = f32[256,256]{1,0:T(8,128)} async-done(((f32[256,256]{1,0:T(8,128)}), f32[256,256]{1,0:T(8,128)}) %all-reduce.7.cloned.1.call-update) | async-done | bytes 262160 | tf_op jit(solution)/shard_map/psum | solution.py:53
  294.0 1.1 fusion.28
  295.0 2.7 convolution_convert_fusion.1
  297.8 21.7 %psum.60 = f32[256,1]{0,1:T(1,128)S(1)} all-reduce(f32[256,1]{0,1:T(1,128)S(1)} %bitcast.89), channel_id=1, replica_groups=mesh['grp'=2,'seq'=8,'mdl'=2] {'seq'}, use_global_device_ids=true, to_apply=%region_10.11 | all-reduce | flops 256 | bytes 2048 | tf_op jit(solution)/shard_map/psum | solution.py:47
  319.5 43.6 %reduce-scatter.9.cloned.1.call-done = bf16[256,256]{1,0:T(8,128)(2,1)} async-done(((bf16[256,2048]{1,0:T(8,128)(2,1)}), bf16[256,256]{1,0:T(8,128)(2,1)}) %reduce-scatter.9.cloned.1.call-update) | async-done | bytes 131088 | tf_op jit(solution)/shard_map/reduce_scatter | solution.py:49
  363.1 1.7 fusion.55
  364.8 0.0 all-reduce.9.cloned.1.call-start
  364.9 39.0 %all-gather.9.cloned.1.call-done = bf16[256,2048]{1,0:T(8,128)(2,1)} async-done(((bf16[256,256]{1,0:T(8,128)(2,1)}), bf16[256,2048]{1,0:T(8,128)(2,1)}) %all-gather.9.cloned.1.call-update) | async-done | bytes 1048592 | tf_op jit(solution)/shard_map/all_gather | solution.py:52
  403.9 2.7 fusion.8
  406.7 17.3 %all-reduce.9.cloned.1.call-done = f32[256,256]{1,0:T(8,128)} async-done(((f32[256,256]{1,0:T(8,128)}), f32[256,256]{1,0:T(8,128)}) %all-reduce.9.cloned.1.call-update) | async-done | bytes 262160 | tf_op jit(solution)/shard_map/psum | solution.py:53
  423.9 1.1 fusion.30
  425.0 2.7 convolution_convert_fusion
  427.7 0.0 all-gather.11.cloned.1.call-start
  427.7 21.7 %psum.62 = f32[256,1]{0,1:T(1,128)S(1)} all-reduce(f32[256,1]{0,1:T(1,128)S(1)} %bitcast.90), channel_id=1, replica_groups=mesh['grp'=2,'seq'=8,'mdl'=2] {'seq'}, use_global_device_ids=true, to_apply=%region_14.15 | all-reduce | flops 256 | bytes 2048 | tf_op jit(solution)/shard_map/psum | solution.py:47
  449.4 43.6 %reduce-scatter.11.cloned.1.call-done = bf16[256,256]{1,0:T(8,128)(2,1)} async-done(((bf16[256,2048]{1,0:T(8,128)(2,1)}), bf16[256,256]{1,0:T(8,128)(2,1)}) %reduce-scatter.11.cloned.1.call-update) | async-done | bytes 131088 | tf_op jit(solution)/shard_map/reduce_scatter | solution.py:49
  493.0 1.7 fusion.63
  494.8 39.0 %all-gather.11.cloned.1.call-done = bf16[256,2048]{1,0:T(8,128)(2,1)} async-done(((bf16[256,256]{1,0:T(8,128)(2,1)}), bf16[256,2048]{1,0:T(8,128)(2,1)}) %all-gather.11.cloned.1.call-update) | async-done | bytes 1048592 | tf_op jit(solution)/shard_map/all_gather | solution.py:52
  533.8 2.7 fusion.5
  536.6 17.3 %all-reduce.11.cloned.1.call-done = f32[256,256]{1,0:T(8,128)} async-done(((f32[256,256]{1,0:T(8,128)}), f32[256,256]{1,0:T(8,128)}) %all-reduce.11.cloned.1.call-update) | async-done | bytes 262160 | tf_op jit(solution)/shard_map/psum | solution.py:53
  553.9 1.6 fusion.31
  555.5 5.8 %all-to-all-start.1 = ((bf16[8,32,256]{2,1,0:T(8,128)(2,1)}), bf16[8,32,256]{2,1,0:T(8,128)(2,1)S(1)}, u32[]{:S(2)}, u32[]{:S(2)}) async-start(bf16[8,32,256]{2,1,0:T(8,128)(2,1)} %bitcast.27), calls=%async_computation.5 | async-start | bytes 262144 | tf_op jit(solution)/shard_map/all_to_all | solution.py:81
  561.3 7.4 %all-to-all-done.1 = bf16[8,32,256]{2,1,0:T(8,128)(2,1)S(1)} async-done(((bf16[8,32,256]{2,1,0:T(8,128)(2,1)}), bf16[8,32,256]{2,1,0:T(8,128)(2,1)S(1)}, u32[]{:S(2)}, u32[]{:S(2)}) %all-to-all-start.1) | async-done | bytes 131104 | tf_op jit(solution)/shard_map/all_to_all | solution.py:81
  568.8 0.1 copy.26
  568.8 0.1 reshape.61
  568.9 0.6 constant_dynamic-slice_fusion
  (34 shorter events, 0.5 us)
Async XLA Ops:
  6.5 12.9 %copy-start = (bf16[64,128,16]{1,2,0:T(8,128)(2,1)S(1)}, bf16[64,128,16]{1,2,0:T(8,128)(2,1)}, u32[]{:S(2)}) copy-start(bf16[64,128,16]{1,2,0:T(8,128)(2,1)} %param.7) | copy-start | bytes 786436
  6.5 96.7 %reduce-scatter.5.cloned.1.call-start = ((), (), s32[]{:S(2)}) async-start(), calls=%async_computation.6 | async-start | bytes 1179648 | tf_op jit(solution)/shard_map/reduce_scatter | solution.py:49
  7.5 9.2 %collective-permute-start = (f32[4,64,128]{2,1,0:T(8,128)S(1)}, f32[4,64,128]{2,1,0:T(8,128)S(1)}, u32[]{:S(2)}, u32[]{:S(2)}) collective-permute-start(f32[4,64,128]{2,1,0:T(8,128)S(1)} %slice.49), channel_id=1, source_target_pairs={{2,0},{4,2},{6,4},{8,6},{10,8},{12,10},{14,12},{3,1},{5,3},{7,5},{... | collective-permute-start | bytes 393224 | tf_op jit(solution)/shard_map/ppermute | solution.py:17
  9.5 7.0 %copy-start.2 = (s32[4]{0:T(128)S(1)}, s32[4]{0:T(128)}, u32[]{:S(2)}) copy-start(s32[4]{0:T(128)} %param.6) | copy-start | bytes 52
  14.3 1.9 copy-start.1
  41.0 103.1 %all-gather.5.cloned.1.call-start = ((), (), s32[]{:S(2)}) async-start(), calls=%async_computation.7 | async-start | bytes 1179648 | tf_op jit(solution)/shard_map/all_gather | solution.py:52
  105.0 59.2 %all-reduce.5.cloned.1.call-start = ((), (), s32[]{:S(2)}) async-start(), calls=%async_computation.8 | async-start | bytes 524288 | tf_op jit(solution)/shard_map/psum | solution.py:53
  146.9 86.4 %reduce-scatter.7.cloned.1.call-start = ((), (), s32[]{:S(2)}) async-start(), calls=%async_computation.9 | async-start | bytes 1179648 | tf_op jit(solution)/shard_map/reduce_scatter | solution.py:49
  167.9 106.0 %all-gather.7.cloned.1.call-start = ((), (), s32[]{:S(2)}) async-start(), calls=%async_computation.10 | async-start | bytes 1179648 | tf_op jit(solution)/shard_map/all_gather | solution.py:52
  235.0 59.0 %all-reduce.7.cloned.1.call-start = ((), (), s32[]{:S(2)}) async-start(), calls=%async_computation.11 | async-start | bytes 524288 | tf_op jit(solution)/shard_map/psum | solution.py:53
  276.7 86.4 %reduce-scatter.9.cloned.1.call-start = ((), (), s32[]{:S(2)}) async-start(), calls=%async_computation.12 | async-start | bytes 1179648 | tf_op jit(solution)/shard_map/reduce_scatter | solution.py:49
  297.7 106.1 %all-gather.9.cloned.1.call-start = ((), (), s32[]{:S(2)}) async-start(), calls=%async_computation.13 | async-start | bytes 1179648 | tf_op jit(solution)/shard_map/all_gather | solution.py:52
  364.8 59.1 %all-reduce.9.cloned.1.call-start = ((), (), s32[]{:S(2)}) async-start(), calls=%async_computation.14 | async-start | bytes 524288 | tf_op jit(solution)/shard_map/psum | solution.py:53
  406.6 86.4 %reduce-scatter.11.cloned.1.call-start = ((), (), s32[]{:S(2)}) async-start(), calls=%async_computation.15 | async-start | bytes 1179648 | tf_op jit(solution)/shard_map/reduce_scatter | solution.py:49
  427.7 106.2 %all-gather.11.cloned.1.call-start = ((), (), s32[]{:S(2)}) async-start(), calls=%async_computation.16 | async-start | bytes 1179648 | tf_op jit(solution)/shard_map/all_gather | solution.py:52
  494.8 59.1 %all-reduce.11.cloned.1.call-start = ((), (), s32[]{:S(2)}) async-start(), calls=%async_computation.17 | async-start | bytes 524288 | tf_op jit(solution)/shard_map/psum | solution.py:53
  555.5 13.2 %all-to-all-start.1 = ((bf16[8,32,256]{2,1,0:T(8,128)(2,1)}), bf16[8,32,256]{2,1,0:T(8,128)(2,1)S(1)}, u32[]{:S(2)}, u32[]{:S(2)}) async-start(bf16[8,32,256]{2,1,0:T(8,128)(2,1)} %bitcast.27), calls=%async_computation.5 | async-start | bytes 262144 | tf_op jit(solution)/shard_map/all_to_all | solution.py:81
Sparse Core Ops, SparseCore 0:
  41.2 62.0 reduce-scatter.4
  105.5 38.5 all-gather.4
  147.0 17.1 all-reduce.4
  168.0 65.1 reduce-scatter.6
  235.3 38.5 all-gather.6
  276.8 17.1 all-reduce.6
  297.8 65.1 reduce-scatter.8
  365.3 38.5 all-gather.8
  406.7 17.1 all-reduce.8
  427.8 65.1 reduce-scatter.10
  495.3 38.5 all-gather.10
  536.7 17.1 all-reduce.10

commit v2 on v1

--- a/solution.py
+++ b/solution.py
@@ -1,9 +1,14 @@
 import math
+from functools import partial
 
 import jax
 import jax.numpy as jnp
 from jax import lax
+from jax.experimental import pallas as pl
+from jax.experimental.pallas import tpu as pltpu
 from jax.sharding import PartitionSpec as P
+
+MESH = pl.DeviceIdType.MESH
 
 HOP = 128
 
@@ -54,6 +59,271 @@
     return (values + added).astype(jnp.bfloat16)
 
 
+def exchange_kernel(
+    sizes,
+    tok_ref, pick_ref, place_ref, up_hbm, down_hbm, out_ref,
+    up_v, down_v, arrived, x_v, sq_v, y_out, y_in, z_out, z_in, hid, pair_out, pair_in, fin_out, fin_in,
+    up_sem, down_sem, in_send, in_recv, sq_send, sq_recv, ys, yr, zs, zr, hzs, hzr, hys, hyr, ps, pr, fs, fr,
+):
+    n, layers, live, dq, fq, width = sizes
+    nz = n // 2
+    s = lax.axis_index("seq")
+    m = lax.axis_index("mdl")
+    z, y = s // 2, s % 2
+    mate = z * 2 + (1 - y)
+    me = s * 2 + m
+
+    loads = []
+    for k in range(layers):
+        loads.append(pltpu.make_async_copy(up_hbm.at[k], up_v.at[k], up_sem.at[k]))
+        loads.append(pltpu.make_async_copy(down_hbm.at[k], down_v.at[k], down_sem.at[k]))
+    for load in loads:
+        load.start()
+    sq_v[...] = jnp.zeros_like(sq_v)
+
+    barrier = pltpu.get_barrier_semaphore()
+    for d in range(1, 2 * n):
+        other = lax.rem(me + d, 2 * n)
+        pl.semaphore_signal(
+            barrier, inc=1, device_id={"seq": other // 2, "mdl": other % 2}, device_id_type=MESH
+        )
+    pl.semaphore_wait(barrier, 2 * n - 1)
+
+    def remote(src, dst, send, recv, seq, mdl):
+        return pltpu.make_async_remote_copy(
+            src_ref=src, dst_ref=dst, send_sem=send, recv_sem=recv,
+            device_id={"seq": seq, "mdl": mdl}, device_id_type=MESH,
+        )
+
+    def token_copy(j, m2):
+        return remote(
+            tok_ref.at[:, j * dq : (j + 1) * dq], arrived.at[s],
+            in_send.at[2 * j + m2], in_recv.at[s], m * nz + j, m2,
+        )
+
+    for j in range(nz):
+        for m2 in range(2):
+            own = ((m * nz + j) * 2 + m2) == me
+
+            @pl.when(jnp.logical_not(own))
+            def _():
+                token_copy(j, m2).start()
+
+            @pl.when(own)
+            def _():
+                pltpu.make_async_copy(
+                    tok_ref.at[:, j * dq : (j + 1) * dq], arrived.at[s], in_recv.at[s]
+                ).start()
+
+    for src in range(n):
+        pltpu.make_async_copy(arrived.at[src], arrived.at[src], in_recv.at[src]).wait()
+    for j in range(nz):
+        for m2 in range(2):
+
+            @pl.when(((m * nz + j) * 2 + m2) != me)
+            def _():
+                token_copy(j, m2).wait_send()
+
+    gathered = arrived[...].reshape(pick_ref.shape[1], dq)
+    x_v[...] = jnp.dot(pick_ref[...], gathered, preferred_element_type=jnp.float32).astype(jnp.bfloat16)
+
+    order = list(range(1, nz)) + [0]
+
+    def layer(k, carry):
+        x = x_v[...]
+        xf = x.astype(jnp.float32)
+        ones = jnp.ones((8, dq), jnp.float32)
+        sq_v[k, 0, :, :live] = lax.dot_general(
+            ones, xf * xf, (((1,), (1,)), ((), ())),
+            precision=lax.Precision.HIGHEST, preferred_element_type=jnp.float32,
+        )
+        sq_copies = [
+            remote(sq_v.at[k, 0], sq_v.at[k, d], sq_send.at[k, d], sq_recv.at[k, d], lax.rem(s + d, n), m)
+            for d in range(1, n)
+        ]
+
+        @pl.when(k < 1)
+        def _():
+            for kk in range(layers):
+                pltpu.make_async_copy(up_hbm.at[kk], up_v.at[kk], up_sem.at[kk]).wait()
+                pltpu.make_async_copy(down_hbm.at[kk], down_v.at[kk], down_sem.at[kk]).wait()
+
+        def up_part(t, col):
+            block = (lax.rem(z + t, nz) * 2 + col) * fq
+            return jnp.dot(
+                x, up_v[k, :, pl.ds(pl.multiple_of(block, fq), fq)], preferred_element_type=jnp.float32
+            )
+
+        y_copies = [
+            remote(y_out.at[t], y_in.at[k, t], ys.at[k, t], yr.at[k, t], mate, m) for t in range(nz)
+        ]
+        for t in order:
+            y_out[t] = up_part(t, 1 - y).astype(jnp.bfloat16)
+            y_copies[t].start()
+            if t == 1:
+                for c in sq_copies:
+                    c.start()
+        z_copies = {
+            t: remote(
+                z_out.at[t], z_in.at[k, t], zs.at[k, t], zr.at[k, t], lax.rem(z + t, nz) * 2 + y, m
+            )
+            for t in range(1, nz)
+        }
+        acc = None
+        for t in order:
+            mine = up_part(t, y)
+            y_copies[t].wait_recv()
+            both = mine + y_in[k, t].astype(jnp.float32)
+            if t:
+                z_out[t] = both.astype(jnp.bfloat16)
+                z_copies[t].start()
+            else:
+                acc = both
+        for c in sq_copies:
+            c.wait_recv()
+        total = sq_v[k, 0]
+        for d in range(1, n):
+            total = total + sq_v[k, d]
+        scale = lax.rsqrt(total * (1.0 / width) + EPSILON)
+        scale = scale.T[:live, :1]
+        for t in range(1, nz):
+            z_copies[t].wait_recv()
+            acc = acc + z_in[k, t].astype(jnp.float32)
+        v = acc * scale
+        hid[k, 0, 0] = (
+            0.5 * v * (1.0 + jnp.tanh(0.7978845608 * (v + 0.044715 * (v * v * v))))
+        ).astype(jnp.bfloat16)
+
+        hz = {
+            t: remote(
+                hid.at[k, 0, 0], hid.at[k, 0, t], hzs.at[k, t], hzr.at[k, t],
+                lax.rem(z + t, nz) * 2 + y, m,
+            )
+            for t in range(1, nz)
+        }
+        hy = [
+            remote(hid.at[k, 0, t], hid.at[k, 1, t], hys.at[k, t], hyr.at[k, t], mate, m)
+            for t in range(nz)
+        ]
+        for t in range(1, nz):
+            hz[t].start()
+        hy[0].start()
+
+        def down_part(t, row, col):
+            block = (lax.rem(z - t + nz, nz) * 2 + col) * fq
+            return lax.dot_general(
+                hid[k, row, t], down_v[k, :, pl.ds(pl.multiple_of(block, fq), fq)],
+                (((1,), (1,)), ((), ())), preferred_element_type=jnp.float32,
+            )
+
+        summed = down_part(0, 0, y)
+        for t in range(1, nz):
+            hz[t].wait_recv()
+            hy[t].start()
+            summed = summed + down_part(t, 0, y)
+        for t in range(nz):
+            hy[t].wait_recv()
+            summed = summed + down_part(t, 1, 1 - y)
+        pair_out[...] = summed
+        pair = remote(pair_out, pair_in.at[k], ps.at[k], pr.at[k], s, 1 - m)
+        pair.start()
+        for c in sq_copies + y_copies + hy + list(z_copies.values()) + list(hz.values()):
+            c.wait_send()
+        pair.wait_recv()
+        x_v[...] = (xf + (summed + pair_in[k])).astype(jnp.bfloat16)
+        pair.wait_send()
+        return carry
+
+    lax.fori_loop(0, layers, layer, 0)
+
+    spread = jnp.dot(place_ref[...], x_v[...], preferred_element_type=jnp.float32).astype(jnp.bfloat16)
+    fin_out[...] = spread.reshape(fin_out.shape)
+    fin_in[0] = fin_out[s]
+    copies = []
+    for d in range(1, n):
+        dest = lax.rem(s + d, n)
+        copies.append(remote(fin_out.at[dest], fin_in.at[d], fs.at[d], fr.at[d], dest, m))
+        copies[-1].start()
+    out_ref[:, pl.ds(pl.multiple_of(s * dq, dq), dq)] = fin_in[0]
+    for d in range(1, n):
+        copies[d - 1].wait_recv()
+        src = lax.rem(s - d + n, n)
+        out_ref[:, pl.ds(pl.multiple_of(src * dq, dq), dq)] = fin_in[d]
+    for c in copies:
+        c.wait_send()
+
+
+def selection(lengths, streams, frames, n, live):
+    total = streams * frames * n
+    spot = jnp.arange(total, dtype=jnp.int32)
+    frame = (spot // (streams * frames)) * frames + spot % frames
+    stream = spot // frames % streams
+    rank = frame
+    limit = jnp.zeros_like(spot)
+    for i in range(streams):
+        rank = rank + jnp.where(stream > i, lengths[i], 0)
+        limit = limit + jnp.where(stream == i, lengths[i], 0)
+    rank = jnp.where(frame < limit, rank, -1)
+    return rank
+
+
+def run_layers(tokens, lengths, up_weight, down_weight, live):
+    streams, frames, half = tokens.shape
+    n = lax.axis_size("seq")
+    layers, dq, ff = up_weight.shape
+    fq = ff // n
+    nz = n // 2
+    width = dq * n
+    rows = streams * frames
+    rank = selection(lengths, streams, frames, n, live)
+    slot = jnp.arange(live, dtype=jnp.int32)
+    pick = (slot[:, None] == rank[None, :]).astype(jnp.bfloat16)
+    kept = lax.dynamic_slice_in_dim(
+        rank.reshape(n, 2, rows // 2), lax.axis_index("mdl"), 1, 1
+    ).reshape(n * rows // 2)
+    place = (kept[:, None] == slot[None, :]).astype(jnp.bfloat16)
+    sizes = (n, layers, live, dq, fq, width)
+    bf, f32, dma = jnp.bfloat16, jnp.float32, pltpu.SemaphoreType.DMA
+    vmem = pl.BlockSpec(memory_space=pltpu.VMEM)
+    lanes = -(-live // 128) * 128
+    out = pl.pallas_call(
+        partial(exchange_kernel, sizes),
+        out_shape=jax.ShapeDtypeStruct((rows // 2, width), bf),
+        in_specs=[vmem, vmem, vmem, pl.BlockSpec(memory_space=pl.ANY), pl.BlockSpec(memory_space=pl.ANY)],
+        out_specs=vmem,
+        scratch_shapes=[
+            pltpu.VMEM((layers, dq, ff), bf),
+            pltpu.VMEM((layers, dq, ff), bf),
+            pltpu.VMEM((n, rows, dq), bf),
+            pltpu.VMEM((live, dq), bf),
+            pltpu.VMEM((layers, n, 8, lanes), f32),
+            pltpu.VMEM((nz, live, fq), bf),
+            pltpu.VMEM((layers, nz, live, fq), bf),
+            pltpu.VMEM((nz, live, fq), bf),
+            pltpu.VMEM((layers, nz, live, fq), bf),
+            pltpu.VMEM((layers, 2, nz, live, fq), bf),
+            pltpu.VMEM((live, dq), f32),
+            pltpu.VMEM((layers, live, dq), f32),
+            pltpu.VMEM((n, rows // 2, dq), bf),
+            pltpu.VMEM((n, rows // 2, dq), bf),
+            dma((layers,)), dma((layers,)),
+            dma((n,)), dma((n,)),
+            dma((layers, n)), dma((layers, n)),
+            dma((layers, nz)), dma((layers, nz)),
+            dma((layers, nz)), dma((layers, nz)),
+            dma((layers, nz)), dma((layers, nz)),
+            dma((layers, nz)), dma((layers, nz)),
+            dma((layers,)), dma((layers,)),
+            dma((n,)), dma((n,)),
+        ],
+        compiler_params=pltpu.CompilerParams(
+            collective_id=0, has_side_effects=True, vmem_limit_bytes=48 * 1024 * 1024
+        ),
+        name="exchange",
+    )(tokens.reshape(rows, half), pick, place, up_weight, down_weight)
+    return out.reshape(streams // 2, frames, width)
+
+
 def body(signal, lengths, chan_weight, up_weight, down_weight):
     streams, channels, samples = signal.shape
     frames = samples // HOP
@@ -70,6 +340,11 @@
         "scfb,cbe->sfce", logpower, chan_weight, preferred_element_type=jnp.float32
     )
     embedded = embedded.reshape(streams, frames, channels * chan_weight.shape[2])
+    shards = lax.axis_size("seq")
+    live = (streams + 1) * frames * shards // 2
+    blocks = (up_weight.shape[1], up_weight.shape[2] // shards)
+    if lax.axis_size("mdl") == 2 and shards % 2 == 0 and all(b % 128 == 0 for b in blocks) and live % 16 == 0:
+        return run_layers(embedded.astype(jnp.bfloat16), lengths, up_weight, down_weight, live)
     frame_index = lax.axis_index("seq") * frames + jnp.arange(frames, dtype=jnp.int32)
     live_mask = frame_index[None, :] < lengths[:, None]
     tokens = jnp.where(live_mask[:, :, None], embedded, 0.0).astype(jnp.bfloat16)

time: 577 us -> 161 us (0.28)
  waiting for transfers between devices: 407 us -> 0.01 us
  Pallas kernels: 0 us -> 140 us
  blocking collectives: 101 us -> 0 us
  matrix products: 27.1 us -> 4.33 us
  between operations: 13.7 us -> 0.19 us
  other arithmetic: 15 us -> 8.49 us
  starting transfers between devices: 7.53 us -> 1.29 us
    reduce_scatter x4 -> x0, waiting for transfers between devices: 174 us -> none  [apply_layer(): summed = lax.psum_scatter(partial, 'seq', scatter_dimension=1, tiled=True)]
    all_gather x4 -> x0, waiting for transfers between devices: 156 us -> none  [apply_layer(): hidden = lax.all_gather(hidden, 'seq', axis=1, tiled=True)]
    pallas_call x0 -> x1, Pallas kernels: none -> 140 us  [run_layers(): pl.pallas_call(partial(exchange_kernel, sizes), out_shape=jax.ShapeDtypeS...]
    psum x4 -> x0, blocking collectives: 83.7 us -> none  [apply_layer(): squares = lax.psum(jnp.sum(values * values, axis=1, keepdims=True), 'seq')]
    psum x4 -> x0, waiting for transfers between devices: 69.1 us -> none  [apply_layer(): added = lax.psum(project_down(hidden, down_rows), 'mdl')]
    dot_general x8 -> x0, matrix products: 21.6 us -> none  [the longest x4 10.9 us: project_down(): lax.dot_general(hidden, own_down, (((1,), (1,)), ((), ())), preferred_ele...]
    all_to_all x1 -> x0, blocking collectives: 15.4 us -> none  [body(): state = lax.all_to_all(rows, 'seq', split_axis=1, concat_axis=0, tiled=True)]
    convert_element_type x6 -> x2, other arithmetic: 8.63 us -> 0.11 us  [the longest x1 0.09 us: run_layers(): place = (kept[:, None] == slot[None, :]).astype(jnp.bfloat16)]
  transfers between devices with their start and end apart: 14 -> 1, of which waited for: 13 -> 0; matrix products, arithmetic and copies ran while one was open for 1% -> 7% of each run, Pallas kernels for 0% -> 0%
where the time goes in v2:
time: 161 us
  Pallas kernels  140 us (87%)
  other arithmetic  8.49 us (5%)
  local copies, waits for them, and re-layouts  6.82 us (4%)
  matrix products  4.33 us (3%)
    pallas_call x1, Pallas kernels, run_layers(): pl.pallas_call(partial(exchange_kernel, sizes), out_shape=jax.ShapeDtypeS...  140 us
    select_n x2, other arithmetic, selection(): rank = jnp.where(frame < limit, rank, -1)  5.19 us
    dot_general x1, matrix products, body(): jnp.dot(signal.reshape(streams, channels, frames, HOP), dft_table, precis...  3.55 us
    unnamed x11, local copies, waits for them, and re-layouts  3.48 us
  transfers between devices with their start and end apart: 1, of which 0 were waited for; matrix products, arithmetic and copies ran while one was open for 7% of the time, Pallas kernels for 0%

profile of v2, /device:TPU:0, one launch (start us, length us, event | category | flops | bytes accessed | tf_op | source)
XLA Modules:
  0.0 161.2 jit_solution(1312941158388029807)
XLA Ops:
  0.0 0.0 copy-start
  0.0 0.0 copy-start.3
  0.0 1.0 slice.41
  1.0 1.3 collective-permute-start
  2.3 0.5 sine_negate_fusion
  3.0 0.1 maximum_multiply_fusion
  3.1 0.0 copy-done.3
  3.1 3.5 %convolution_bitcast_fusion = f32[4,64,8,512]{3,1,2,0:T(8,128)S(1)} fusion(f32[128,256]{1,0:T(8,128)S(1)} %get-tuple-element.6, f32[128,256]{1,0:T(8,128)S(1)} %get-tuple-element.5, f32[4,64,1024]{2,1,0:T(8,128)S(1)} %copy-done.3), kind=kOutput, calls=%fused_computation | convolution fusion | flops 1610678272 | bytes 5505024 | tf_op jit(solution)/shard_map/dot_general | solution.py:332
  6.7 0.0 copy-start.2
  6.7 0.0 copy-start.4
  6.7 0.2 slice.51
  7.0 0.4 copy-done.4
  7.4 1.1 fusion.42
  8.4 0.2 copy-done.2
  8.7 2.6 %compare_select_fusion.6 = s32[256]{0:T(256)S(1)} fusion(s32[]{:T(128)} %bitcast.12, s32[]{:T(128)} %bitcast.11, s32[]{:T(128)} %bitcast.10, s32[]{:T(128)} %bitcast.9), kind=kLoop, calls=%fused_computation.69 | loop fusion | flops 14336 | bytes 1040 | tf_op jit(solution)/shard_map/jit(_where)/select_n | solution.py:266
  11.3 2.6 %add_select_fusion.5 = s32[8,1,16]{2,0,1:T(8,128)S(1)} fusion(s32[8,2,16]{2,0,1:T(8,128)S(1)} %get-tuple-element.14, s32[]{:T(128)S(6)} %select_n.241, s32[8,2,16]{2,0,1:T(8,128)S(1)} %fusion.21, pred[8,2,16]{2,0,1:T(8,128)(4,1)S(1)} %get-tuple-element.15, pred[8,2,16]{2,0,1:T(8,128)(4,1)S(1)} %broadcast_compare_fusion.2, ...), kind=kLoop, calls=%fused_computation.54 | loop fusion | flops 2944 | bytes 2452 | tf_op jit(solution)/shard_map/jit(_where)/select_n | solution.py:266
  13.9 0.1 eq.84
  14.0 0.1 fusion.18.place_ref
  14.1 0.0 collective-permute-done
  14.1 0.4 convolution_bitcast_fusion.1
  14.5 2.0 %slice_add_fusion = f32[4,64,8,256]{3,1,2,0:T(8,128)S(1)} fusion(f32[4,64,8,512]{3,1,2,0:T(8,128)} %copy-done.2, f32[4,64,1,256]{3,1,2,0:T(8,128)S(1)} %convolution_bitcast_fusion.1, f32[4,64,7,256]{3,1,2,0:T(8,128)S(1)} %slice.51), kind=kLoop, calls=%fused_computation.1 | loop fusion | flops 1048576 | bytes 6291456 | tf_op jit(solution)/shard_map/add | solution.py:337
  16.4 0.4 fusion.5
  16.9 0.0 copy-done
  16.9 0.4 fusion
  17.3 0.2 copy.11
  17.5 0.8 convert_element_type.36.tok_ref
  18.3 0.0 copy-start.1
  18.3 2.2 %copy-done.1 = bf16[4,256,2048]{2,1,0:T(8,128)(2,1)S(1)} copy-done((bf16[4,256,2048]{2,1,0:T(8,128)(2,1)S(1)}, bf16[4,256,2048]{2,1,0:T(8,128)(2,1)}, u32[]{:S(2)}) %copy-start.1) | copy-done | bytes 4194328
  20.5 140.0 %exchange.1 = bf16[16,2048]{1,0:T(8,128)(2,1)S(1)} custom-call(bf16[32,1024]{1,0:T(8,128)(2,1)S(1)} %convert_element_type.36.tok_ref, bf16[160,256]{1,0:T(8,128)(2,1)S(1)} %fusion.10.pick_ref, bf16[128,160]{1,0:T(8,128)(2,1)S(1)} %fusion.18.place_ref, bf16[4,256,2048]{2,1,0:T(8,128)(2,1)S(1)} %copy-done.1, bf16[4,256,2048]{2,1,0:T(8,128)(2,1)} %down_hbm.1), custom_call_target="tpu_custom_call" | custom-call | tf_op jit(solution)/shard_map/exchange/pallas_call | solution.py:289
  160.5 0.6 copy.22
  (7 shorter events, 0.2 us)
Async XLA Ops:
  0.0 16.9 %copy-start = (bf16[64,128,16]{1,2,0:T(8,128)(2,1)S(1)}, bf16[64,128,16]{1,2,0:T(8,128)(2,1)}, u32[]{:S(2)}) copy-start(bf16[64,128,16]{1,2,0:T(8,128)(2,1)} %param.7) | copy-start | bytes 786436
  0.0 3.1 %copy-start.3 = (f32[4,64,1024]{2,1,0:T(8,128)S(1)}, f32[4,64,1024]{2,1,0:T(8,128)}, u32[]{:S(2)}) copy-start(f32[4,64,1024]{2,1,0:T(8,128)} %param.5) | copy-start | bytes 3145732
  1.0 13.0 %collective-permute-start = (f32[4,64,128]{2,1,0:T(8,128)S(1)}, f32[4,64,128]{2,1,0:T(8,128)S(1)}, u32[]{:S(2)}, u32[]{:S(2)}) collective-permute-start(f32[4,64,128]{2,1,0:T(8,128)S(1)} %slice.41), channel_id=1, source_target_pairs={{2,0},{4,2},{6,4},{8,6},{10,8},{12,10},{14,12},{3,1},{5,3},{7,5},{... | collective-permute-start | bytes 393224 | tf_op jit(solution)/shard_map/ppermute | solution.py:22
  6.7 1.9 %copy-start.2 = (f32[4,64,8,512]{3,1,2,0:T(8,128)}, f32[4,64,8,512]{3,1,2,0:T(8,128)S(1)}, u32[]{:S(2)}) copy-start(f32[4,64,8,512]{3,1,2,0:T(8,128)S(1)} %convolution_bitcast_fusion) | copy-start | bytes 12582916
  6.7 0.7 copy-start.4
  18.3 2.2 %copy-start.1 = (bf16[4,256,2048]{2,1,0:T(8,128)(2,1)S(1)}, bf16[4,256,2048]{2,1,0:T(8,128)(2,1)}, u32[]{:S(2)}) copy-start(bf16[4,256,2048]{2,1,0:T(8,128)(2,1)} %up_hbm.1) | copy-start | bytes 12582916

commit v3 on v1

--- a/solution.py
+++ b/solution.py
@@ -1,9 +1,15 @@
 import math
+from functools import partial
 
 import jax
 import jax.numpy as jnp
 from jax import lax
+from jax.experimental import pallas as pl
+from jax.experimental.pallas import tpu as pltpu
 from jax.sharding import PartitionSpec as P
+
+MESH = pl.DeviceIdType.MESH
+CHUNKS = 2
 
 HOP = 128
 
@@ -54,6 +60,293 @@
     return (values + added).astype(jnp.bfloat16)
 
 
+def exchange_kernel(
+    sizes,
+    len_ref, tok_ref, up_hbm, down_hbm, out_ref,
+    up_v, down_v, arrived, x_v, sq_v, y_out, y_in, z_out, z_in, hid, pair_out, pair_in, fin_out, fin_in,
+    up_sem, down_sem, in_send, in_recv, ys, yr, zs, zr, hzs, hzr, hys, hyr, ps, pr, fs, fr,
+):
+    n, layers, streams, frames, live, dq, fq, width = sizes
+    nz = n // 2
+    rows = streams * frames
+    ch = live // CHUNKS
+    s = lax.axis_index("seq")
+    m = lax.axis_index("mdl")
+    z, y = s // 2, s % 2
+    mate = z * 2 + (1 - y)
+    me = s * 2 + m
+
+    def rank_of(stream, frame):
+        rank, limit = frame, jnp.zeros_like(frame)
+        for i in range(streams):
+            rank = rank + jnp.where(stream > i, len_ref[i], 0)
+            limit = limit + jnp.where(stream == i, len_ref[i], 0)
+        return jnp.where(frame < limit, rank, -1)
+
+    loads = []
+    for k in range(layers):
+        loads.append(pltpu.make_async_copy(up_hbm.at[k], up_v.at[k], up_sem.at[k]))
+        loads.append(pltpu.make_async_copy(down_hbm.at[k], down_v.at[k], down_sem.at[k]))
+    for load in loads:
+        load.start()
+    y_out[...] = jnp.zeros_like(y_out)
+    z_out[...] = jnp.zeros_like(z_out)
+    sq_v[...] = jnp.zeros_like(sq_v)
+
+    barrier = pltpu.get_barrier_semaphore()
+    for d in range(1, 2 * n):
+        other = lax.rem(me + d, 2 * n)
+        pl.semaphore_signal(
+            barrier, inc=1, device_id={"seq": other // 2, "mdl": other % 2}, device_id_type=MESH
+        )
+    pl.semaphore_wait(barrier, 2 * n - 1)
+
+    def remote(src, dst, send, recv, seq, mdl):
+        return pltpu.make_async_remote_copy(
+            src_ref=src, dst_ref=dst, send_sem=send, recv_sem=recv,
+            device_id={"seq": seq, "mdl": mdl}, device_id_type=MESH,
+        )
+
+    def token_copy(j, m2):
+        return remote(
+            tok_ref.at[:, j * dq : (j + 1) * dq], arrived.at[s],
+            in_send.at[2 * j + m2], in_recv.at[s], m * nz + j, m2,
+        )
+
+    for j in range(nz):
+        for m2 in range(2):
+            own = ((m * nz + j) * 2 + m2) == me
+
+            @pl.when(jnp.logical_not(own))
+            def _():
+                token_copy(j, m2).start()
+
+            @pl.when(own)
+            def _():
+                pltpu.make_async_copy(
+                    tok_ref.at[:, j * dq : (j + 1) * dq], arrived.at[s], in_recv.at[s]
+                ).start()
+
+    for src in range(n):
+        pltpu.make_async_copy(arrived.at[src], arrived.at[src], in_recv.at[src]).wait()
+    for j in range(nz):
+        for m2 in range(2):
+
+            @pl.when(((m * nz + j) * 2 + m2) != me)
+            def _():
+                token_copy(j, m2).wait_send()
+
+    spot = lax.broadcasted_iota(jnp.int32, (1, n * rows), 1)
+    rank = rank_of(spot // frames % streams, spot // rows * frames + spot % frames)
+    slot = lax.broadcasted_iota(jnp.int32, (live, n * rows), 0)
+    pick = jnp.where(slot == rank, 1.0, 0.0).astype(jnp.bfloat16)
+    gathered = arrived[...].reshape(n * rows, dq)
+    x_v[...] = (
+        jnp.dot(pick, gathered, preferred_element_type=jnp.float32)
+        .astype(jnp.bfloat16)
+        .reshape(CHUNKS, ch, dq)
+    )
+    for load in loads:
+        load.wait()
+
+    order = list(range(1, nz)) + [0]
+    tail = sq_v.shape[-1]
+
+    def up_part(k, x, t, col):
+        block = (lax.rem(z + t, nz) * 2 + col) * fq
+        return jnp.dot(
+            x, up_v[k, :, pl.ds(pl.multiple_of(block, fq), fq)], preferred_element_type=jnp.float32
+        )
+
+    def y_copy(k, c, t):
+        i = k * CHUNKS + c
+        return remote(y_out.at[c, t], y_in.at[i, t], ys.at[i, t], yr.at[i, t], mate, m)
+
+    def z_copy(k, c, t):
+        i = k * CHUNKS + c
+        return remote(
+            z_out.at[c, t], z_in.at[i, t], zs.at[i, t], zr.at[i, t], lax.rem(z + t, nz) * 2 + y, m
+        )
+
+    def hz_copy(k, c, t):
+        i = k * CHUNKS + c
+        return remote(
+            hid.at[i, 0, 0], hid.at[i, 0, t], hzs.at[i, t], hzr.at[i, t], lax.rem(z + t, nz) * 2 + y, m
+        )
+
+    def hy_copy(k, c, t):
+        i = k * CHUNKS + c
+        return remote(hid.at[i, 0, t], hid.at[i, 1, t], hys.at[i, t], hyr.at[i, t], mate, m)
+
+    def pair_copy(k, c):
+        i = k * CHUNKS + c
+        return remote(pair_out.at[c], pair_in.at[i], ps.at[i], pr.at[i], s, 1 - m)
+
+    def send_up(k, c):
+        x = x_v[c]
+        xf = x.astype(jnp.float32)
+        squares = lax.dot_general(
+            jnp.ones((16, dq), jnp.float32), xf * xf, (((1,), (1,)), ((), ())),
+            precision=lax.Precision.HIGHEST, preferred_element_type=jnp.float32,
+        )
+        sq_v[c, :, :ch] = squares
+        for t in order:
+            y_out[c, t, :ch] = up_part(k, x, t, 1 - y).astype(jnp.bfloat16)
+            y_out[c, t, ch:, :ch] = squares.astype(jnp.bfloat16)
+            y_copy(k, c, t).start()
+
+    def combine(k, c):
+        i = k * CHUNKS + c
+        x = x_v[c]
+        for t in order:
+            mine = up_part(k, x, t, y)
+            y_copy(k, c, t).wait_recv()
+            both = mine + y_in[i, t, :ch].astype(jnp.float32)
+            squares = sq_v[c] + y_in[i, t, ch:, :tail].astype(jnp.float32)
+            if t:
+                z_out[c, t, :ch] = both.astype(jnp.bfloat16)
+                z_out[c, t, ch:, :tail] = squares.astype(jnp.bfloat16)
+                z_copy(k, c, t).start()
+        return both, squares
+
+    def activate(k, c, both, squares):
+        i = k * CHUNKS + c
+        for t in range(1, nz):
+            z_copy(k, c, t).wait_recv()
+            both = both + z_in[i, t, :ch].astype(jnp.float32)
+            squares = squares + z_in[i, t, ch:, :tail].astype(jnp.float32)
+        scale = lax.rsqrt(squares * (1.0 / width) + EPSILON).T[:ch, :1]
+        v = both * scale
+        hid[i, 0, 0] = (
+            0.5 * v * (1.0 + jnp.tanh(0.7978845608 * (v + 0.044715 * (v * v * v))))
+        ).astype(jnp.bfloat16)
+        for t in range(1, nz):
+            hz_copy(k, c, t).start()
+        hy_copy(k, c, 0).start()
+
+    def down_part(k, c, t, row, col):
+        block = (lax.rem(z - t + nz, nz) * 2 + col) * fq
+        return lax.dot_general(
+            hid[k * CHUNKS + c, row, t], down_v[k, :, pl.ds(pl.multiple_of(block, fq), fq)],
+            (((1,), (1,)), ((), ())), preferred_element_type=jnp.float32,
+        )
+
+    def forward(k, c):
+        summed = down_part(k, c, 0, 0, y)
+        for t in range(1, nz):
+            hz_copy(k, c, t).wait_recv()
+            hy_copy(k, c, t).start()
+            summed = summed + down_part(k, c, t, 0, y)
+        return summed
+
+    def finish(k, c, summed):
+        for t in range(nz):
+            hy_copy(k, c, t).wait_recv()
+            summed = summed + down_part(k, c, t, 1, 1 - y)
+        pair_out[c] = summed
+        pair_copy(k, c).start()
+        for t in range(nz):
+            y_copy(k, c, t).wait_send()
+            hy_copy(k, c, t).wait_send()
+        for t in range(1, nz):
+            z_copy(k, c, t).wait_send()
+            hz_copy(k, c, t).wait_send()
+        pair_copy(k, c).wait_recv()
+        x_v[c] = (x_v[c].astype(jnp.float32) + (summed + pair_in[k * CHUNKS + c])).astype(jnp.bfloat16)
+        pair_copy(k, c).wait_send()
+
+        @pl.when(k + 1 < layers)
+        def _():
+            send_up(k + 1, c)
+
+    for c in range(CHUNKS):
+        send_up(0, c)
+
+    def layer(k, carry):
+        parts = [combine(k, c) for c in range(CHUNKS)]
+        for c in range(CHUNKS):
+            activate(k, c, *parts[c])
+        sums = [forward(k, c) for c in range(CHUNKS)]
+        for c in range(CHUNKS):
+            finish(k, c, sums[c])
+        return carry
+
+    lax.fori_loop(0, layers, layer, 0)
+
+    half = rows // 2
+    spot = lax.broadcasted_iota(jnp.int32, (n * half, 1), 0)
+    rank = rank_of(m * (streams // 2) + spot // frames % (streams // 2), spot // half * frames + spot % frames)
+    slot = lax.broadcasted_iota(jnp.int32, (n * half, live), 1)
+    place = jnp.where(slot == rank, 1.0, 0.0).astype(jnp.bfloat16)
+    spread = jnp.dot(place, x_v[...].reshape(live, dq), preferred_element_type=jnp.float32).astype(jnp.bfloat16)
+    fin_out[...] = spread.reshape(fin_out.shape)
+    fin_in[0] = fin_out[s]
+    copies = []
+    for d in range(1, n):
+        dest = lax.rem(s + d, n)
+        copies.append(remote(fin_out.at[dest], fin_in.at[d], fs.at[d], fr.at[d], dest, m))
+        copies[-1].start()
+    out_ref[:, pl.ds(pl.multiple_of(s * dq, dq), dq)] = fin_in[0]
+    for d in range(1, n):
+        copies[d - 1].wait_recv()
+        src = lax.rem(s - d + n, n)
+        out_ref[:, pl.ds(pl.multiple_of(src * dq, dq), dq)] = fin_in[d]
+    for c in copies:
+        c.wait_send()
+
+
+def run_layers(tokens, lengths, up_weight, down_weight, live):
+    streams, frames, half = tokens.shape
+    n = lax.axis_size("seq")
+    layers, dq, ff = up_weight.shape
+    fq = ff // n
+    nz = n // 2
+    width = dq * n
+    rows = streams * frames
+    sizes = (n, layers, streams, frames, live, dq, fq, width)
+    ch = live // CHUNKS
+    slots = layers * CHUNKS
+    bf, f32, dma = jnp.bfloat16, jnp.float32, pltpu.SemaphoreType.DMA
+    vmem = pl.BlockSpec(memory_space=pltpu.VMEM)
+    hbm = pl.BlockSpec(memory_space=pltpu.HBM)
+    lanes = -(-ch // 128) * 128
+    out = pl.pallas_call(
+        partial(exchange_kernel, sizes),
+        out_shape=jax.ShapeDtypeStruct((rows // 2, width), bf),
+        in_specs=[pl.BlockSpec(memory_space=pltpu.SMEM), vmem, hbm, hbm],
+        out_specs=vmem,
+        scratch_shapes=[
+            pltpu.VMEM((layers, dq, ff), bf),
+            pltpu.VMEM((layers, dq, ff), bf),
+            pltpu.VMEM((n, rows, dq), bf),
+            pltpu.VMEM((CHUNKS, ch, dq), bf),
+            pltpu.VMEM((CHUNKS, 16, lanes), f32),
+            pltpu.VMEM((CHUNKS, nz, ch + 16, fq), bf),
+            pltpu.VMEM((slots, nz, ch + 16, fq), bf),
+            pltpu.VMEM((CHUNKS, nz, ch + 16, fq), bf),
+            pltpu.VMEM((slots, nz, ch + 16, fq), bf),
+            pltpu.VMEM((slots, 2, nz, ch, fq), bf),
+            pltpu.VMEM((CHUNKS, ch, dq), f32),
+            pltpu.VMEM((slots, ch, dq), f32),
+            pltpu.VMEM((n, rows // 2, dq), bf),
+            pltpu.VMEM((n, rows // 2, dq), bf),
+            dma((layers,)), dma((layers,)),
+            dma((n,)), dma((n,)),
+            dma((slots, nz)), dma((slots, nz)),
+            dma((slots, nz)), dma((slots, nz)),
+            dma((slots, nz)), dma((slots, nz)),
+            dma((slots, nz)), dma((slots, nz)),
+            dma((slots,)), dma((slots,)),
+            dma((n,)), dma((n,)),
+        ],
+        compiler_params=pltpu.CompilerParams(
+            collective_id=0, has_side_effects=True, vmem_limit_bytes=48 * 1024 * 1024
+        ),
+        name="exchange",
+    )(lengths, tokens.reshape(rows, half), up_weight, down_weight)
+    return out.reshape(streams // 2, frames, width)
+
+
 def body(signal, lengths, chan_weight, up_weight, down_weight):
     streams, channels, samples = signal.shape
     frames = samples // HOP
@@ -70,6 +363,11 @@
         "scfb,cbe->sfce", logpower, chan_weight, preferred_element_type=jnp.float32
     )
     embedded = embedded.reshape(streams, frames, channels * chan_weight.shape[2])
+    shards = lax.axis_size("seq")
+    live = (streams + 1) * frames * shards // 2
+    blocks = (up_weight.shape[1], up_weight.shape[2] // shards)
+    if lax.axis_size("mdl") == 2 and shards % 2 == 0 and all(b % 128 == 0 for b in blocks) and live % (16 * CHUNKS) == 0 and live // CHUNKS <= blocks[1]:
+        return run_layers(embedded.astype(jnp.bfloat16), lengths, up_weight, down_weight, live)
     frame_index = lax.axis_index("seq") * frames + jnp.arange(frames, dtype=jnp.int32)
     live_mask = frame_index[None, :] < lengths[:, None]
     tokens = jnp.where(live_mask[:, :, None], embedded, 0.0).astype(jnp.bfloat16)

time: 577 us -> 133 us (0.23)
  waiting for transfers between devices: 407 us -> 2.47 us
  Pallas kernels: 0 us -> 118 us
  blocking collectives: 101 us -> 0 us
  matrix products: 27.1 us -> 4.4 us
  between operations: 13.7 us -> 0.13 us
  other arithmetic: 15 us -> 1.55 us
  starting transfers between devices: 7.53 us -> 1.29 us
    reduce_scatter x4 -> x0, waiting for transfers between devices: 174 us -> none  [apply_layer(): summed = lax.psum_scatter(partial, 'seq', scatter_dimension=1, tiled=True)]
    all_gather x4 -> x0, waiting for transfers between devices: 156 us -> none  [apply_layer(): hidden = lax.all_gather(hidden, 'seq', axis=1, tiled=True)]
    pallas_call x0 -> x1, Pallas kernels: none -> 118 us  [run_layers(): pl.pallas_call(partial(exchange_kernel, sizes), out_shape=jax.ShapeDtypeS...]
    psum x4 -> x0, blocking collectives: 83.7 us -> none  [apply_layer(): squares = lax.psum(jnp.sum(values * values, axis=1, keepdims=True), 'seq')]
    psum x4 -> x0, waiting for transfers between devices: 69.1 us -> none  [apply_layer(): added = lax.psum(project_down(hidden, down_rows), 'mdl')]
    dot_general x8 -> x0, matrix products: 21.6 us -> none  [the longest x4 10.9 us: project_down(): lax.dot_general(hidden, own_down, (((1,), (1,)), ((), ())), preferred_ele...]
    all_to_all x1 -> x0, blocking collectives: 15.4 us -> none  [body(): state = lax.all_to_all(rows, 'seq', split_axis=1, concat_axis=0, tiled=True)]
    convert_element_type x6 -> x0, other arithmetic: 8.63 us -> none  [the longest x4 6.91 us: apply_layer(): jax.nn.gelu(summed.astype(jnp.float32) * scale).astype(jnp.bfloat16)]
  transfers between devices with their start and end apart: 14 -> 1, of which waited for: 13 -> 1; matrix products, arithmetic and copies ran while one was open for 1% -> 3% of each run, Pallas kernels for 0% -> 0%
where the time goes in v3:
time: 133 us
  Pallas kernels  118 us (89%)
  local copies, waits for them, and re-layouts  5.06 us (4%)
  matrix products  4.4 us (3%)
  waiting for transfers between devices  2.47 us (2%)
  other arithmetic  1.55 us (1%)
    pallas_call x1, Pallas kernels, run_layers(): pl.pallas_call(partial(exchange_kernel, sizes), out_shape=jax.ShapeDtypeS...  118 us
    dot_general x1, matrix products, body(): jnp.dot(signal.reshape(streams, channels, frames, HOP), dft_table, precis...  3.62 us
    unnamed x9, local copies, waits for them, and re-layouts  2.83 us
  transfers between devices with their start and end apart: 1, of which 1 were waited for; matrix products, arithmetic and copies ran while one was open for 3% of the time, Pallas kernels for 0%

profile of v3, /device:TPU:0, one launch (start us, length us, event | category | flops | bytes accessed | tf_op | source)
XLA Modules:
  0.0 133.0 jit_solution(15075635398758690449)
XLA Ops:
  0.0 0.0 copy-start
  0.0 0.0 copy-start.3
  0.0 1.0 slice.25
  1.0 1.3 collective-permute-start
  2.4 0.5 sine_negate_fusion
  2.9 0.1 maximum_multiply_fusion
  3.0 0.0 copy-done.3
  3.1 3.6 %convolution_bitcast_fusion = f32[4,64,8,512]{3,1,2,0:T(8,128)S(1)} fusion(f32[128,256]{1,0:T(8,128)S(1)} %get-tuple-element.6, f32[128,256]{1,0:T(8,128)S(1)} %get-tuple-element.5, f32[4,64,1024]{2,1,0:T(8,128)S(1)} %copy-done.3), kind=kOutput, calls=%fused_computation | convolution fusion | flops 1610678272 | bytes 5505024 | tf_op jit(solution)/shard_map/dot_general | solution.py:355
  6.7 0.2 slice.31
  6.9 2.5 %collective-permute-done = f32[4,64,128]{2,1,0:T(8,128)S(1)} collective-permute-done((f32[4,64,128]{2,1,0:T(8,128)S(1)}, f32[4,64,128]{2,1,0:T(8,128)S(1)}, u32[]{:S(2)}, u32[]{:S(2)}) %collective-permute-start) | collective-permute-done | bytes 131104 | tf_op jit(solution)/shard_map/ppermute | solution.py:23
  9.4 0.4 convolution_bitcast_fusion.1
  9.8 0.4 slice_add_fusion
  10.2 0.4 fusion.5
  10.7 0.0 copy-done
  10.7 0.0 copy-start.2
  10.7 0.4 fusion
  11.1 0.2 copy.11
  11.3 0.8 convert_element_type.30.tok_ref
  12.1 0.0 copy-done.2
  12.1 0.0 copy-start.1
  12.1 2.2 %copy-done.1 = bf16[4,256,2048]{2,1,0:T(8,128)(2,1)S(1)} copy-done((bf16[4,256,2048]{2,1,0:T(8,128)(2,1)S(1)}, bf16[4,256,2048]{2,1,0:T(8,128)(2,1)}, u32[]{:S(2)}) %copy-start.1) | copy-done | bytes 4194328
  14.3 118.1 %exchange.1 = bf16[16,2048]{1,0:T(8,128)(2,1)S(1)} custom-call(s32[4]{0:T(128)S(1)} %copy-done.2, bf16[32,1024]{1,0:T(8,128)(2,1)S(1)} %convert_element_type.30.tok_ref, bf16[4,256,2048]{2,1,0:T(8,128)(2,1)S(1)} %copy-done.1, bf16[4,256,2048]{2,1,0:T(8,128)(2,1)} %down_hbm.1), custom_call_target="tpu_custom_call" | custom-call | tf_op jit(solution)/shard_map/exchange/pallas_call | solution.py:313
  132.4 0.6 copy.22
  (2 shorter events, 0.1 us)
Async XLA Ops:
  0.0 10.7 %copy-start = (bf16[64,128,16]{1,2,0:T(8,128)(2,1)S(1)}, bf16[64,128,16]{1,2,0:T(8,128)(2,1)}, u32[]{:S(2)}) copy-start(bf16[64,128,16]{1,2,0:T(8,128)(2,1)} %param.7) | copy-start | bytes 786436
  0.0 3.0 %copy-start.3 = (f32[4,64,1024]{2,1,0:T(8,128)S(1)}, f32[4,64,1024]{2,1,0:T(8,128)}, u32[]{:S(2)}) copy-start(f32[4,64,1024]{2,1,0:T(8,128)} %param.5) | copy-start | bytes 3145732
  1.0 8.4 %collective-permute-start = (f32[4,64,128]{2,1,0:T(8,128)S(1)}, f32[4,64,128]{2,1,0:T(8,128)S(1)}, u32[]{:S(2)}, u32[]{:S(2)}) collective-permute-start(f32[4,64,128]{2,1,0:T(8,128)S(1)} %slice.25), channel_id=1, source_target_pairs={{2,0},{4,2},{6,4},{8,6},{10,8},{12,10},{14,12},{3,1},{5,3},{7,5},{... | collective-permute-start | bytes 393224 | tf_op jit(solution)/shard_map/ppermute | solution.py:23
  10.7 1.4 %copy-start.2 = (s32[4]{0:T(128)S(1)}, s32[4]{0:T(128)}, u32[]{:S(2)}) copy-start(s32[4]{0:T(128)} %len_ref.1) | copy-start | bytes 52
  12.1 2.2 %copy-start.1 = (bf16[4,256,2048]{2,1,0:T(8,128)(2,1)S(1)}, bf16[4,256,2048]{2,1,0:T(8,128)(2,1)}, u32[]{:S(2)}) copy-start(bf16[4,256,2048]{2,1,0:T(8,128)(2,1)} %up_hbm.1) | copy-start | bytes 12582916

commit v4 on v3

--- a/solution.py
+++ b/solution.py
@@ -3,6 +3,7 @@
 
 import jax
 import jax.numpy as jnp
+import numpy as np
 from jax import lax
 from jax.experimental import pallas as pl
 from jax.experimental.pallas import tpu as pltpu
@@ -25,14 +26,15 @@
 
 def spectral_table(half_span):
     full_span = 2 * half_span
-    row_index = jnp.arange(full_span, dtype=jnp.int32)
-    col_index = jnp.arange(half_span, dtype=jnp.int32)
-    phases = row_index[:, None] * col_index[None, :] % full_span
-    angles = phases.astype(jnp.float32) * (2.0 * math.pi / full_span)
-    window_taper = 0.5 - 0.5 * jnp.cos(row_index.astype(jnp.float32) * (2.0 * math.pi / full_span))
+    row_index = np.arange(full_span)
+    phases = row_index[:, None] * np.arange(half_span)[None, :] % full_span
+    angles = phases * (2.0 * math.pi / full_span)
+    window_taper = 0.5 - 0.5 * np.cos(row_index * (2.0 * math.pi / full_span))
     weighting = window_taper * (1.0 / math.sqrt(full_span))
-    joined = jnp.concatenate([jnp.cos(angles), -jnp.sin(angles)], axis=1) * weighting[:, None]
-    return jnp.concatenate([joined[:half_span], joined[half_span:]], axis=1)
+    joined = np.concatenate([np.cos(angles), -np.sin(angles)], axis=1) * weighting[:, None]
+    return jnp.asarray(
+        np.concatenate([joined[:half_span], joined[half_span:]], axis=1).astype(np.float32)
+    )
 
 
 def log_power(spectrum):
@@ -74,6 +76,7 @@
     m = lax.axis_index("mdl")
     z, y = s // 2, s % 2
     mate = z * 2 + (1 - y)
+    inner = (z == 1) | (z == 2)
     me = s * 2 + m
 
     def rank_of(stream, frame):
@@ -170,8 +173,13 @@
 
     def hz_copy(k, c, t):
         i = k * CHUNKS + c
+        if nz == 4 and t == 2:
+            source = jnp.where(inner, jnp.where(z == 1, 3, 1), 0)
+            target = jnp.where(inner, jnp.where(z == 1, 0, 3), lax.rem(z + t, nz))
+        else:
+            source, target = 0, lax.rem(z + t, nz)
         return remote(
-            hid.at[i, 0, 0], hid.at[i, 0, t], hzs.at[i, t], hzr.at[i, t], lax.rem(z + t, nz) * 2 + y, m
+            hid.at[i, 0, source], hid.at[i, 0, t], hzs.at[i, t], hzr.at[i, t], target * 2 + y, m
         )
 
     def hy_copy(k, c, t):
@@ -221,7 +229,14 @@
             0.5 * v * (1.0 + jnp.tanh(0.7978845608 * (v + 0.044715 * (v * v * v))))
         ).astype(jnp.bfloat16)
         for t in range(1, nz):
-            hz_copy(k, c, t).start()
+            if nz == 4 and t == 2:
+
+                @pl.when(jnp.logical_not(inner))
+                def _():
+                    hz_copy(k, c, t).start()
+
+            else:
+                hz_copy(k, c, t).start()
         hy_copy(k, c, 0).start()
 
     def down_part(k, c, t, row, col):
@@ -233,8 +248,14 @@
 
     def forward(k, c):
         summed = down_part(k, c, 0, 0, y)
-        for t in range(1, nz):
+        for t in (1, 3, 2) if nz == 4 else range(1, nz):
             hz_copy(k, c, t).wait_recv()
+            if nz == 4 and t != 2:
+
+                @pl.when(z == (2 if t == 1 else 1))
+                def _():
+                    hz_copy(k, c, 2).start()
+
             hy_copy(k, c, t).start()
             summed = summed + down_part(k, c, t, 0, y)
         return summed
@@ -340,7 +361,7 @@
             dma((n,)), dma((n,)),
         ],
         compiler_params=pltpu.CompilerParams(
-            collective_id=0, has_side_effects=True, vmem_limit_bytes=48 * 1024 * 1024
+            collective_id=0, has_side_effects=True, vmem_limit_bytes=60 * 1024 * 1024
         ),
         name="exchange",
     )(lengths, tokens.reshape(rows, half), up_weight, down_weight)
@@ -353,9 +374,9 @@
     dft_table = spectral_table(HOP)
     boundary = shifted(signal[:, :, :HOP], "seq", -1)
     local_part = jnp.dot(
-        signal.reshape(streams, channels, frames, HOP), dft_table, precision=lax.Precision.HIGHEST
-    )
-    edge_part = jnp.dot(boundary, dft_table[:, 2 * HOP :], precision=lax.Precision.HIGHEST)
+        signal.reshape(streams, channels, frames, HOP), dft_table, precision=lax.Precision.HIGH
+    )
+    edge_part = jnp.dot(boundary, dft_table[:, 2 * HOP :], precision=lax.Precision.HIGH)
     following = jnp.concatenate([local_part[:, :, 1:, 2 * HOP :], edge_part[:, :, None, :]], axis=2)
     spectrum = local_part[..., : 2 * HOP] + following
     logpower = log_power(spectrum)

time: 133 us -> 133 us (level)
    unnamed x9 -> x5, local copies, waits for them, and re-layouts: 2.83 us -> 1.48 us
where the time goes in v4:
time: 133 us; the launch traced here: 132 us
  Pallas kernels  118 us (89%)
  local copies, waits for them, and re-layouts  4.26 us (3%)
  matrix products  3.77 us (3%)
  waiting for transfers between devices  3.7 us (3%)
    pallas_call x1, Pallas kernels, run_layers(): pl.pallas_call(partial(exchange_kernel, sizes), out_shape=jax.ShapeDtypeS...  118 us
    ppermute x1, waiting for transfers between devices, shifted(): return lax.ppermute(x, axis, pairs)  3.7 us
    dot_general x1, matrix products, body(): jnp.dot(signal.reshape(streams, channels, frames, HOP), dft_table, precis...  3.1 us
  transfers between devices with their start and end apart: 1, of which 1 were waited for; matrix products, arithmetic and copies ran while one was open for 3% of the time, Pallas kernels for 0%

profile of v4, /device:TPU:0, one launch (start us, length us, event | category | flops | bytes accessed | tf_op | source)
XLA Modules:
  0.0 132.5 jit_solution(15161527775542189392)
XLA Ops:
  0.0 0.0 copy-start
  0.0 1.0 slice.20
  1.0 1.3 collective-permute-start
  2.3 3.1 %convolution_bitcast_fusion = f32[4,64,8,512]{3,1,2,0:T(8,128)S(1)} fusion(f32[128,512,1,1]{1,0,3,2:T(8,128)} %constant.4, f32[4,64,1024]{2,1,0:T(8,128)} %param.6), kind=kOutput, calls=%fused_computation | convolution fusion | flops 805306368 | bytes 5505024 | tf_op jit(solution)/shard_map/dot_general | solution.py:376
  5.4 0.0 copy-start.1
  5.4 0.2 slice.25
  5.6 3.7 %collective-permute-done = f32[4,64,128]{2,1,0:T(8,128)S(1)} collective-permute-done((f32[4,64,128]{2,1,0:T(8,128)S(1)}, f32[4,64,128]{2,1,0:T(8,128)S(1)}, u32[]{:S(2)}, u32[]{:S(2)}) %collective-permute-start) | collective-permute-done | bytes 131104 | tf_op jit(solution)/shard_map/ppermute | solution.py:24
  9.3 0.0 copy-done.1
  9.3 0.3 convolution_bitcast_fusion.1
  9.6 0.4 slice_add_fusion
  10.0 0.4 fusion.5
  10.5 0.0 copy-done
  10.5 0.4 fusion
  10.9 0.2 copy.12
  11.1 1.4 %convert_element_type.16.tok_ref = bf16[32,1024]{1,0:T(8,128)(2,1)} reshape(bf16[4,8,64,16]{3,2,1,0:T(8,128)(2,1)S(1)} %copy.12) | data formatting | bytes 131072 | tf_op jit(solution)/shard_map/convert_element_type | solution.py:391
  12.5 118.5 %exchange.1 = bf16[16,2048]{1,0:T(8,128)(2,1)} custom-call(s32[4]{0:T(128)} %len_ref.1, bf16[32,1024]{1,0:T(8,128)(2,1)} %convert_element_type.16.tok_ref, bf16[4,256,2048]{2,1,0:T(8,128)(2,1)} %up_hbm.1, bf16[4,256,2048]{2,1,0:T(8,128)(2,1)} %down_hbm.1), custom_call_target="tpu_custom_call" | custom-call | tf_op jit(solution)/shard_map/exchange/pallas_call | solution.py:334
  131.0 1.5 %copy.23 = bf16[2,8,2048]{2,1,0:T(8,128)(2,1)} copy(bf16[2,8,2048]{2,1,0:T(8,128)(2,1)} %bitcast.30) | data formatting | bytes 131072
Async XLA Ops:
  0.0 10.5 %copy-start = (bf16[64,128,16]{1,2,0:T(8,128)(2,1)S(1)}, bf16[64,128,16]{1,2,0:T(8,128)(2,1)}, u32[]{:S(2)}) copy-start(bf16[64,128,16]{1,2,0:T(8,128)(2,1)} %param.8) | copy-start | bytes 786436
  1.0 8.4 %collective-permute-start = (f32[4,64,128]{2,1,0:T(8,128)S(1)}, f32[4,64,128]{2,1,0:T(8,128)S(1)}, u32[]{:S(2)}, u32[]{:S(2)}) collective-permute-start(f32[4,64,128]{2,1,0:T(8,128)S(1)} %slice.20), channel_id=1, source_target_pairs={{2,0},{4,2},{6,4},{8,6},{10,8},{12,10},{14,12},{3,1},{5,3},{7,5},{... | collective-permute-start | bytes 393224 | tf_op jit(solution)/shard_map/ppermute | solution.py:24
  5.4 4.0 %copy-start.1 = (f32[128,256,1]{1,0,2:T(8,128)S(1)}, f32[128,256,1]{1,0,2:T(8,128)}, u32[]{:S(2)}) copy-start(f32[128,256,1]{1,0,2:T(8,128)} %constant.5) | copy-start | bytes 393220
